TPU v7x, 32 devices: a whole 2x2x4 slice. The times are simulated.
32 devices in a mesh: outer: 8 (over z, x), inner: 4 (over y, core).
Axes of the slice: x: 2, y: 2, z: 4, core: 2. Of those that a mesh axis runs over, the one named last changes fastest.
Arguments:
- inputs: bfloat16 [16384, 512], P(('outer', 'inner')), may hold values from -6 to 6
- weights: bfloat16 [3151872], replicated
- cotangent: bfloat16 [16384, 512], P(('outer', 'inner')), may hold values from -6 to 6
- clip_lengths: int32 [11], replicated, may hold values from 1 to 1500, 16384 in all
- first_moment: float32 [3151872], P('inner')
- second_moment: float32 [3151872], P('inner')
Outputs:
- layer_output: bfloat16 [16384, 512], P(('outer', 'inner'))
- input_grad: bfloat16 [16384, 512], P(('outer', 'inner'))
- weight_grads: float32 [3151872], P('inner')
- grad_norm: float32 [], replicated
- moment_one: float32 [3151872], P('inner')
- moment_two: float32 [3151872], P('inner')
- weight_step: bfloat16 [3151872], replicated
Inputs may be any that keep to these rules, and one draw needn't show every extreme that they name: `clip_lengths`: the lengths add up to 16384; clip c occupies the slots from the sum of the lengths before it on, in order.
All inputs are finite; a program needn't handle non-finite values.
Results may differ from a plain program's by a relative error of at most 0.015.
Values may be sent and summed in bfloat16 or wider, within the bound.
No kernel may reach another device: no remote copies, remote signals or barrier semaphores. Data moves between devices by JAX's collectives and lax.ppermute only.
A program may use at most 192 MiB of HBM per device.

v0:
```python
import functools
import math

import jax
import jax.numpy as jnp
from jax import lax
from jax.experimental import pallas as pl
from jax.experimental.pallas import tpu as pltpu
from jax.sharding import PartitionSpec as P

D = 512
FF = 2048
MOST = 1500


BETA_ONE = 0.9
BETA_TWO = 0.999
FIX_ONE = 1.0 - (0.9**10) ** 10
FIX_TWO = 1.0 - (0.999**10) ** 10
DECAY = 0.1
INV_ROOT_TWO = 1.0 / math.sqrt(2.0)
INV_ROOT_TWO_PI = 1.0 / math.sqrt(2.0 * math.pi)


def layouts():
    return [
        (D,),
        (D,),
        (D, D),
        (D,),
        (D, D),
        (D, D),
        (D,),
        (D, D),
        (D,),
        (D,),
        (D,),
        (D, FF),
        (FF,),
        (FF, D),
        (D,),
    ]


def plain_dot(matrix_one, matrix_two):
    return jnp.dot(matrix_one, matrix_two, preferred_element_type=jnp.float32)


def rows_dot(matrix_one, matrix_two):
    return lax.dot_general(
        matrix_one, matrix_two, (((0,), (0,)), ((), ())), preferred_element_type=jnp.float32
    )


def back_dot(matrix_one, matrix_two):
    return lax.dot_general(
        matrix_one, matrix_two, (((1,), (1,)), ((), ())), preferred_element_type=jnp.float32
    )


def standard(values):
    center = jnp.mean(values, axis=-1, keepdims=True)
    centered = values - center
    inverse_dev = lax.rsqrt(jnp.mean(centered * centered, axis=-1, keepdims=True) + 1e-05)
    return (centered * inverse_dev, inverse_dev)


def norm_back(grad_normed, normed_hat, inverse_dev, gain):
    scaled = grad_normed * gain
    return inverse_dev * (
        scaled
        - jnp.mean(scaled, axis=-1, keepdims=True)
        - normed_hat * jnp.mean(scaled * normed_hat, axis=-1, keepdims=True)
    )


def bounds(positions, clip_lengths):
    starts = jnp.cumsum(clip_lengths, dtype=jnp.int32) - clip_lengths
    member = (
        jnp.sum((positions[:, None] >= starts[None, :]).astype(jnp.int32), axis=1, dtype=jnp.int32)
        - 1
    )
    onehot = (
        jnp.arange(clip_lengths.shape[0], dtype=jnp.int32)[None, :] == member[:, None]
    ).astype(jnp.int32)
    lower_slot = jnp.sum(onehot * starts[None, :], axis=1, dtype=jnp.int32)
    upper_slot = lower_slot + jnp.sum(onehot * clip_lengths[None, :], axis=1, dtype=jnp.int32)
    return (lower_slot, upper_slot)


LINE = ("outer", "inner")
NEG = -1e30
BRIEF = pl.CostEstimate(flops=1000, bytes_accessed=1000, transcendentals=0)


def shifted(block, distance):
    n = lax.axis_size(LINE)
    return lax.ppermute(block, LINE, [(i + distance, i) for i in range(n) if 0 <= i + distance < n])


def swapped(block, bit):
    n = lax.axis_size(LINE)
    return lax.ppermute(block, LINE, [(i ^ bit, i) for i in range(n)])


def halo(block, before=()):
    n = lax.axis_size(LINE)
    left = shifted(block, -2)
    right = shifted(block, 2)
    partner = swapped(block, 1)
    route = [(i + (3 if i % 2 else -3), i) for i in range(n)]
    far = lax.ppermute(block, LINE, [(s, t) for s, t in route if 0 <= s < n])
    passed_left, passed_right, *_ = lax.optimization_barrier((left, right, *before))
    turned = [swapped(passed_left, 1), swapped(passed_right, 1)]
    return [block, partner, left, right, *turned, far]


def slot_table():
    odd = lax.axis_index(LINE) % 2
    even_slots = jnp.array([6, 2, 4, 0, 1, 3, 5], jnp.int32)
    odd_slots = jnp.array([4, 2, 1, 0, 5, 3, 6], jnp.int32)
    return jnp.where(odd == 1, odd_slots, even_slots)


def dot_nt(a, b):
    return lax.dot_general(a, b, (((1,), (1,)), ((), ())), preferred_element_type=jnp.float32)


def head_halves(pair):
    first = lax.broadcasted_iota(jnp.int32, pair.shape, 1) < pair.shape[1] // 2
    zero = jnp.zeros_like(pair)
    return jnp.where(first, pair, zero), jnp.where(first, zero, pair)


def over_lanes(tile, op):
    parts = [tile[:, 128 * j : 128 * (j + 1)] for j in range(tile.shape[1] // 128)]
    while len(parts) > 1:
        rest = parts[len(parts) // 2 * 2 :]
        parts = [op(parts[2 * j], parts[2 * j + 1]) for j in range(len(parts) // 2)] + rest
    return parts[0]


def tile_mask(block, shape, low, high):
    place = block * shape[1] + lax.broadcasted_iota(jnp.int32, shape, 1)
    return (place >= low) & (place < high)


def forward_kernel(rows_at, first_ref, last_ref, slot_ref, q_ref, k_ref, v_ref, low_ref, high_ref, o_ref, lse_ref, s_ref):
    width = q_ref.shape[0]
    for i in range(width // rows_at):
        rows = pl.ds(i * rows_at, rows_at)
        queries = head_halves(q_ref[rows, :] * jnp.bfloat16(0.125))
        low, high = low_ref[rows, :], high_ref[rows, :]

        def scores(block, peaks):
            keys = k_ref[pl.ds(pl.multiple_of(slot_ref[block] * width, width), width), :]
            mask = tile_mask(block, (rows_at, width), low, high)
            found = []
            for h in range(2):
                score = jnp.where(mask, dot_nt(queries[h], keys), NEG)
                s_ref[h, block] = score
                found.append(jnp.maximum(peaks[h], over_lanes(score, jnp.maximum)))
            return tuple(found)

        start = jnp.full((rows_at, 128), NEG, jnp.float32)
        peaks = lax.fori_loop(first_ref[i], last_ref[i], scores, (start, start))
        peaks = [jnp.max(peak, axis=1, keepdims=True) for peak in peaks]

        def mix(block, carried):
            values = v_ref[pl.ds(pl.multiple_of(slot_ref[block] * width, width), width), :]
            totals, sums = [], []
            for h in range(2):
                soft = jnp.exp(s_ref[h, block] - peaks[h])
                totals.append(carried[0][h] + over_lanes(soft, jnp.add))
                sums.append(carried[1][h] + jnp.dot(soft.astype(jnp.bfloat16), values, preferred_element_type=jnp.float32))
            return tuple(totals), tuple(sums)

        zero = jnp.zeros((rows_at, 128), jnp.float32)
        totals, sums = lax.fori_loop(first_ref[i], last_ref[i], mix, ((zero, zero), (zero, zero)))
        totals = [jnp.sum(total, axis=1, keepdims=True) for total in totals]
        even = lax.broadcasted_iota(jnp.int32, (rows_at, 128), 1) < 64
        o_ref[rows, :] = jnp.where(even, sums[0] / totals[0], sums[1] / totals[1])
        lse_ref[rows, :] = jnp.where(even, peaks[0] + jnp.log(totals[0]), peaks[1] + jnp.log(totals[1]))


def query_kernel(
    rows_at, first_ref, last_ref, slot_ref, q_ref, k_ref, v_ref, g_ref, lse_ref, delta_ref, low_ref, high_ref, dq_ref
):
    width = q_ref.shape[0]
    for i in range(width // rows_at):
        rows = pl.ds(i * rows_at, rows_at)
        queries = head_halves(q_ref[rows, :] * jnp.bfloat16(0.125))
        grads = head_halves(g_ref[rows, :])
        low, high = low_ref[rows, :], high_ref[rows, :]
        lse = [lse_ref[rows, 64 * h : 64 * h + 1] for h in range(2)]
        delta = [delta_ref[rows, 64 * h : 64 * h + 1] for h in range(2)]

        def step(block, carried):
            at = pl.ds(pl.multiple_of(slot_ref[block] * width, width), width)
            keys, values = k_ref[at, :], v_ref[at, :]
            mask = tile_mask(block, (rows_at, width), low, high)
            found = []
            for h in range(2):
                soft = jnp.exp(jnp.where(mask, dot_nt(queries[h], keys) - lse[h], NEG))
                grad = (soft * (dot_nt(grads[h], values) - delta[h])).astype(jnp.bfloat16)
                found.append(carried[h] + jnp.dot(grad, keys, preferred_element_type=jnp.float32))
            return tuple(found)

        zero = jnp.zeros((rows_at, 128), jnp.float32)
        sums = lax.fori_loop(first_ref[i], last_ref[i], step, (zero, zero))
        even = lax.broadcasted_iota(jnp.int32, (rows_at, 128), 1) < 64
        dq_ref[rows, :] = (jnp.where(even, sums[0], sums[1]) * 0.125).astype(jnp.bfloat16)


def key_kernel(
    rows_at, first_ref, last_ref, slot_ref, k_ref, v_ref, q_ref, g_ref, low_ref, high_ref, dk_ref, dv_ref
):
    width = k_ref.shape[0]
    sent = width + stat_rows(width)
    for i in range(width // rows_at):
        rows = pl.ds(i * rows_at, rows_at)
        keys = head_halves(k_ref[rows, :] * jnp.bfloat16(0.125))
        values = head_halves(v_ref[rows, :])
        low, high = low_ref[rows, :], high_ref[rows, :]

        def step(block, carried):
            slot = slot_ref[block]
            at = pl.ds(pl.multiple_of(slot * width, width), width)
            queries = q_ref[at, :]
            grads = g_ref[pl.ds(pl.multiple_of(slot * sent, 16), width), :]
            packed = g_ref[pl.ds(pl.multiple_of(slot * sent + width, 16), sent - width), :].astype(jnp.float32)
            mask = tile_mask(block, (rows_at, width), low, high)
            key_sums, value_sums = [], []
            for h in range(2):
                lse = unpacked_stat(packed, h, width)
                delta = unpacked_stat(packed, 2 + h, width)
                soft = jnp.exp(jnp.where(mask, dot_nt(keys[h], queries) - lse, NEG))
                value_sums.append(
                    carried[1][h] + jnp.dot(soft.astype(jnp.bfloat16), grads, preferred_element_type=jnp.float32)
                )
                grad = (soft * (dot_nt(values[h], grads) - delta)).astype(jnp.bfloat16)
                key_sums.append(carried[0][h] + jnp.dot(grad, queries, preferred_element_type=jnp.float32))
            return tuple(key_sums), tuple(value_sums)

        zero = jnp.zeros((rows_at, 128), jnp.float32)
        key_sums, value_sums = lax.fori_loop(first_ref[i], last_ref[i], step, ((zero, zero), (zero, zero)))
        even = lax.broadcasted_iota(jnp.int32, (rows_at, 128), 1) < 64
        dk_ref[rows, :] = (jnp.where(even, key_sums[0], key_sums[1]) * 0.125).astype(jnp.bfloat16)
        dv_ref[rows, :] = jnp.where(even, value_sums[0], value_sums[1]).astype(jnp.bfloat16)


def stat_rows(width):
    return -(-12 * (width // 128) // 16) * 16


def unpacked_stat(packed, which, width):
    pieces = width // 128
    parts = []
    for j in range(pieces):
        at = [(3 * which + part) * pieces + j for part in range(3)]
        parts.append(packed[at[0] : at[0] + 1] + packed[at[1] : at[1] + 1] + packed[at[2] : at[2] + 1])
    return jnp.concatenate(parts, axis=1)


def mixed_grad_kernel(branch_ref, weight_ref, mixed_ref, lse_ref, sent_ref, delta_ref):
    width = branch_ref.shape[0]
    grad = dot_nt(branch_ref[...], weight_ref[...]).astype(jnp.bfloat16)
    sent_ref[pl.ds(0, width), :] = grad
    product = grad.astype(jnp.float32) * mixed_ref[...]
    even = lax.broadcasted_iota(jnp.int32, product.shape, 1) < 64
    sums = [jnp.sum(part, axis=1, keepdims=True) for part in head_halves(product)]
    delta = jnp.where(even, sums[0], sums[1])
    delta_ref[...] = delta
    rows = []
    for kept in (lse_ref[...], delta):
        turned = kept.T
        for h in range(2):
            row = turned[64 * h : 64 * h + 1, :]
            for _ in range(3):
                part = row.astype(jnp.bfloat16).astype(jnp.float32)
                row = row - part
                rows.extend(part[:, 128 * j : 128 * (j + 1)] for j in range(width // 128))
    spare = stat_rows(width) - len(rows)
    if spare:
        rows.append(jnp.zeros((spare, 128), jnp.float32))
    sent_ref[pl.ds(width, stat_rows(width)), :] = jnp.concatenate(rows, axis=0).astype(jnp.bfloat16)


def mixed_grad(branch, out_weight, mixed, lse):
    width = branch.shape[0]
    column = pl.BlockSpec((width, 128), lambda h: (0, h))
    return pl.pallas_call(
        mixed_grad_kernel,
        name="mixed_grad",
        grid=(D // 128,),
        in_specs=[
            pl.BlockSpec((width, D), lambda h: (0, 0)),
            pl.BlockSpec((128, D), lambda h: (h, 0)),
            column,
            column,
        ],
        out_specs=[pl.BlockSpec((width + stat_rows(width), 128), lambda h: (0, h)), column],
        out_shape=[
            jax.ShapeDtypeStruct((width + stat_rows(width), D), jnp.bfloat16),
            jax.ShapeDtypeStruct((width, D), jnp.float32),
        ],
        cost_estimate=BRIEF,
    )(branch, out_weight, mixed, lse)


ROWS_AT = 256


def attend(kernel, ranges, operands, results, scratch, pairs=(0, D // 128), after=()):
    begin, count = pairs
    specs = []
    for array, (kind, at) in operands:
        if kind == "own":
            specs.append(pl.BlockSpec((ranges[3], 128), lambda h, *_, at=at + begin: (0, at + h)))
        elif kind == "window":
            specs.append(pl.BlockSpec((array.shape[0], 128), lambda h, *_, at=at + begin: (0, at + h)))
        else:
            specs.append(pl.BlockSpec(array.shape, lambda h, *_, n=array.ndim: (0,) * n))
    tok_rows = ranges[3]
    return pl.pallas_call(
        functools.partial(kernel, ROWS_AT),
        grid_spec=pltpu.PrefetchScalarGridSpec(
            num_scalar_prefetch=3,
            grid=(count,),
            in_specs=specs,
            out_specs=[pl.BlockSpec((tok_rows, 128), lambda h, *_: (0, h))] * len(results),
            scratch_shapes=scratch,
        ),
        out_shape=[jax.ShapeDtypeStruct((tok_rows, 128 * count), kept) for kept in results],
        compiler_params=pltpu.CompilerParams(vmem_limit_bytes=48 * 2**20),
        cost_estimate=BRIEF,
    )(*[behind(bound, after) for bound in ranges[:1]], *ranges[1:3], *[array for array, _ in operands])


VECTOR = pltpu.VMEM
ANY = pl.ANY


def behind(value, others):
    return lax.optimization_barrier((value, *others))[0]


def halves_rows(shard_rows):
    return -(-shard_rows // 128) * 64


def unpack_kernel(plan, shard_rows, flat_ref, *refs):
    wide_ref = refs[-1]
    padded_ref = refs[-2]
    total = flat_ref.shape[0]
    chunk = 432

    def widen(i, _):
        rows = pl.ds(pl.multiple_of(i * chunk, 16), chunk)
        wide_ref[rows, :] = flat_ref[rows, :].astype(jnp.float32)
        return 0

    lax.fori_loop(0, total // chunk, widen, 0)
    wide_ref[pl.ds(total, wide_ref.shape[0] - total), :] = jnp.zeros((wide_ref.shape[0] - total, 128), jnp.float32)
    for (offset, rows, columns, begin), ref in zip(plan, refs[:-2]):
        pieces = columns // 128
        if rows == 1:
            for j in range(pieces):
                ref[:, 128 * j : 128 * (j + 1)] = wide_ref[pl.ds(offset + j, 1), :]
            continue

        def matrix(i, _):
            at = pl.multiple_of(i * 64, 64)
            for j in range(pieces):
                part = wide_ref[pl.ds(offset + j + at * pieces, 64, stride=pieces), :]
                ref[pl.ds(at, 64), begin + 128 * j : begin + 128 * (j + 1)] = part.astype(jnp.bfloat16)
            return 0

        lax.fori_loop(0, rows // 64, matrix, 0)
    shards = total // shard_rows
    half = halves_rows(shard_rows)
    for s in range(shards):
        for h in range(2):

            def pad(i, _):
                part = wide_ref[pl.ds(s * shard_rows + h * half + i * 64, 64), :]
                padded_ref[s * 2 + h, pl.ds(pl.multiple_of(i * 64, 64), 64), :] = part.astype(jnp.bfloat16)
                return 0

            lax.fori_loop(0, half // 64, pad, 0)


def unpacked(weights, shard_rows):
    flat = weights.reshape(-1, 128)
    half = halves_rows(shard_rows)
    plan, outs = [], []
    offset = 0
    for layout in layouts():
        rows, columns = layout if len(layout) == 2 else (1, layout[0])
        plan.append([offset, rows, columns, 0])
        outs.append(jax.ShapeDtypeStruct((rows, columns), jnp.bfloat16 if rows > 1 else jnp.float32))
        offset = offset + rows * columns // 128
    shards = flat.shape[0] // shard_rows
    outs.append(jax.ShapeDtypeStruct((2 * shards, half, 128), jnp.bfloat16))
    return pl.pallas_call(
        functools.partial(unpack_kernel, plan, shard_rows),
        name="unpack",
        in_specs=[pl.BlockSpec(memory_space=VECTOR)],
        out_specs=[pl.BlockSpec(memory_space=VECTOR)] * len(outs),
        out_shape=outs,
        scratch_shapes=[VECTOR((flat.shape[0] + 2 * half, 128), jnp.float32)],
        compiler_params=pltpu.CompilerParams(vmem_limit_bytes=60 * 2**20),
        cost_estimate=BRIEF,
    )(flat)


def pack_kernel(plan, spans, place_ref, *refs):
    count = len(plan)
    keep_ref, give_ref, flat_ref, out_ref, sems = refs[-5:]
    end = max(offset + rows * columns // 128 for offset, rows, columns in plan)
    begin = min(offset for offset, _, _ in plan)
    if begin:
        flat_ref[pl.ds(0, begin), :] = jnp.zeros((begin, 128), jnp.float32)
    for (offset, rows, columns), ref in zip(plan, refs[:count]):
        pieces = columns // 128
        if rows == 1:
            for j in range(pieces):
                flat_ref[pl.ds(offset + j, 1), :] = ref[:, 128 * j : 128 * (j + 1)]
            continue

        def matrix(i, _):
            at = pl.multiple_of(i * 64, 64)
            for j in range(pieces):
                flat_ref[pl.ds(offset + j + at * pieces, 64, stride=pieces), :] = ref[pl.ds(at, 64), 128 * j : 128 * (j + 1)]
            return 0

        lax.fori_loop(0, rows // 64, matrix, 0)
    for h in range(2):
        at = h ^ place_ref[0]
        filled = 0
        for source, rows, room in spans[h]:
            whole = rows // 64

            def move(i, _):
                to = pl.ds(pl.multiple_of(filled + i * 64, 16), 64)
                out_ref[at, to, :] = flat_ref[pl.ds(source + i * 64, 64), :].astype(jnp.bfloat16)
                return 0

            lax.fori_loop(0, whole, move, 0)
            rest = rows - 64 * whole
            tail = room - 64 * whole
            if tail:
                parts = []
                if rest:
                    parts.append(flat_ref[pl.ds(source + 64 * whole, rest), :])
                if tail > rest:
                    parts.append(jnp.zeros((tail - rest, 128), jnp.float32))
                last = parts[0] if len(parts) == 1 else jnp.concatenate(parts, axis=0)
                out_ref[at, pl.ds(filled + 64 * whole, tail), :] = last.astype(jnp.bfloat16)
            filled = filled + room
    copies = [
        pltpu.make_async_copy(out_ref.at[0], keep_ref, sems.at[0]),
        pltpu.make_async_copy(out_ref.at[1], give_ref, sems.at[1]),
    ]
    for copy in copies:
        copy.start()
    for copy in copies:
        copy.wait()


def packed_halves(grads, begin, spans, half):
    plan = []
    offset = begin
    for grad in grads:
        plan.append((offset, *grad.shape))
        offset = offset + grad.shape[0] * grad.shape[1] // 128
    return pl.pallas_call(
        functools.partial(pack_kernel, plan, spans),
        name="pack",
        in_specs=[pl.BlockSpec(memory_space=pltpu.SMEM)] + [pl.BlockSpec(memory_space=VECTOR)] * len(grads),
        out_specs=[pl.BlockSpec(memory_space=ANY)] * 2,
        out_shape=[jax.ShapeDtypeStruct((half, 128), jnp.bfloat16)] * 2,
        scratch_shapes=[
            VECTOR((offset, 128), jnp.float32),
            VECTOR((2, half, 128), jnp.bfloat16),
            pltpu.SemaphoreType.DMA((2,)),
        ],
        compiler_params=pltpu.CompilerParams(vmem_limit_bytes=60 * 2**20),
        cost_estimate=BRIEF,
    )(bit_of(1).reshape(1), *grads)


def combine_kernel(count, places_ref, *refs):
    parts, outs = refs[:count], refs[-places_ref.shape[0] :]
    rows = outs[0].shape[0]
    for k, out in enumerate(outs):
        at = pl.ds(pl.multiple_of(places_ref[k] * rows, 16), rows)
        terms = [part[at, :].astype(jnp.float32) for part in parts]
        while len(terms) > 1:
            terms = [terms[2 * j] + terms[2 * j + 1] for j in range(len(terms) // 2)]
        out[...] = terms[0].astype(jnp.bfloat16)


def places_of(group):
    if not group:
        return jnp.zeros((1,), jnp.int32)
    place = (lax.axis_index(LINE) // group[0]) % (1 << len(group))
    return place ^ jnp.arange(1 << len(group), dtype=jnp.int32)


def combine(parts, group, after):
    count = 1 << len(group)
    rows = parts[0].shape[0] // count
    outs = pl.pallas_call(
        functools.partial(combine_kernel, len(parts)),
        name="combine",
        in_specs=[pl.BlockSpec(memory_space=pltpu.SMEM)]
        + [pl.BlockSpec(memory_space=VECTOR)] * len(parts),
        out_specs=[pl.BlockSpec(memory_space=VECTOR)] * count,
        out_shape=[jax.ShapeDtypeStruct((rows, 128), jnp.bfloat16)] * count,
        cost_estimate=BRIEF,
    )(behind(places_of(group), after), *parts)
    return list(outs)


def stack_kernel(count, places_ref, *refs):
    out_ref = refs[-1]
    rows = refs[0].shape[0]
    for k in range(count):
        out_ref[pl.ds(pl.multiple_of(places_ref[k] * rows, 16), rows), :] = refs[k][...]


def stack(parts, group, after):
    rows = parts[0].shape[0] * len(parts)
    return pl.pallas_call(
        functools.partial(stack_kernel, len(parts)),
        name="stack",
        in_specs=[pl.BlockSpec(memory_space=pltpu.SMEM)]
        + [pl.BlockSpec(memory_space=VECTOR)] * len(parts),
        out_specs=pl.BlockSpec(memory_space=VECTOR),
        out_shape=jax.ShapeDtypeStruct((rows, 128), jnp.bfloat16),
        cost_estimate=BRIEF,
    )(behind(places_of(group), after), *parts)


def exchanged(parts, group):
    return [parts[0]] + [swapped(parts[k % len(parts)], group[0] * k) for k in range(1, 1 << len(group))]


def bit_groups():
    bits = [1 << k for k in range(1, lax.axis_size(LINE).bit_length() - 1)]
    return [bits[k : k + 2] for k in range(0, len(bits), 2)]


def update_kernel(
    shards, late, shard_rows, meta_ref, scale_ref, early_own, early_other, late_own, late_other, extra_own, extra_other,
    weight_ref, one_ref, two_ref, *refs
):
    moments = refs[: 2 * shards]
    step_ref, grad_ref, new_one_ref, new_two_ref, sum_ref, wide_ref, stage_ref, sems = refs[2 * shards :]
    which, k = pl.program_id(0), pl.program_id(1)
    core, me, turn = meta_ref[0], meta_ref[1], meta_ref[2]
    shard = me ^ k
    half = core ^ which
    rows = sum_ref.shape[0]
    chunk = rows // 7 if rows % 112 == 0 else 64
    scale = scale_ref[0]

    def by_chunks(body):
        def move(i, _):
            body(pl.multiple_of(i * chunk, 16))
            return 0

        lax.fori_loop(0, rows // chunk, move, 0)

    def load(ref):
        def body(at):
            sum_ref[pl.ds(at, chunk), :] = ref[pl.ds(at, chunk), :].astype(jnp.float32) * scale

        by_chunks(body)

    for array, side, is_late in ((early_own, 0, 0), (early_other, 1, 0), (late_own, 0, 1), (late_other, 1, 1)):
        pl.when((which == side) & ((shard < late) == (is_late == 1)))(functools.partial(load, array))
    for array, side in ((extra_own, 0), (extra_other, 1)):

        @pl.when((which == side) & (shard == late) & (half == 0))
        def _():
            sum_ref[pl.ds(0, 8), :] = sum_ref[pl.ds(0, 8), :] + array[pl.ds(0, 8), :].astype(jnp.float32) * scale

    def moved(clipped, one, two):
        one = BETA_ONE * one + (1.0 - BETA_ONE) * clipped
        two = BETA_TWO * two + (1.0 - BETA_TWO) * clipped * clipped
        return one, two

    base = shard * shard_rows + half * rows
    limit = jnp.where(half == 1, shard_rows - rows, rows)
    for j in range(shards):

        @pl.when(k == j)
        def _():
            def body(start):
                at = pl.ds(start, chunk)
                first, second = moments[2 * j][at, :], moments[2 * j + 1][at, :]
                one, two = jnp.where(turn == 1, second, first), jnp.where(turn == 1, first, second)
                one, two = moved(sum_ref[at, :], one.astype(jnp.float32), two.astype(jnp.float32))
                update = (one * (1.0 / FIX_ONE)) / (jnp.sqrt(two * (1.0 / FIX_TWO)) + 1e-08)
                update = update + DECAY * weight_ref[0, at, :].astype(jnp.float32)
                to = pl.ds(base + start, chunk)
                inside = start + lax.broadcasted_iota(jnp.int32, update.shape, 0) < limit
                wide_ref[to, :] = jnp.where(inside, update, wide_ref[to, :])

            by_chunks(body)

    @pl.when(k == 0)
    def _():
        unscale = scale_ref[1]

        def body(start):
            at = pl.ds(start, chunk)
            clipped = sum_ref[at, :]
            one, two = moved(clipped, one_ref[at, :], two_ref[at, :])
            grad_ref[at, :] = clipped * unscale
            new_one_ref[at, :] = one
            new_two_ref[at, :] = two

        by_chunks(body)

    @pl.when((which == 1) & (k == shards - 1))
    def _():
        piece = stage_ref.shape[1]
        total = step_ref.shape[0]

        def sending(i, slot):
            return pltpu.make_async_copy(
                stage_ref.at[slot], step_ref.at[pl.ds(pl.multiple_of(i * piece, 16), piece), :], sems.at[slot]
            )

        count = total // piece
        for i in range(count):
            if i >= 2:
                sending(i - 2, i % 2).wait()
            stage_ref[i % 2] = wide_ref[pl.ds(i * piece, piece), :].astype(jnp.bfloat16)
            sending(i, i % 2).start()
        for i in range(count - 2, count):
            sending(i, i % 2).wait()


def updated(norm, early, late, late_shards, weights, first_moment, second_moment, moments):
    shards = len(moments) // 2
    rows = weights.shape[1]
    shard_rows = first_moment.shape[0] // 128
    line = lax.axis_index(LINE)
    inner = lax.axis_size("inner")
    meta = jnp.stack([line % 2, lax.axis_index("inner"), (line // inner) % 2]).astype(jnp.int32)
    last = shards - 1

    def early_map(side):
        def index(w, k, meta):
            k = jnp.where(w == side, k, last if side == 0 else 0)
            return (jnp.clip((meta[1] ^ k) - late_shards, 0, shards - late_shards - 1), 0)

        return index

    def late_map(side):
        def index(w, k, meta):
            k = jnp.where(w == side, k, last if side == 0 else 0)
            return (jnp.clip(meta[1] ^ k, 0, late_shards - 1), 0)

        return index

    by_half = pl.BlockSpec((rows, 128), lambda w, k, meta: (meta[0] ^ w, 0))
    by_shard = pl.BlockSpec((1, rows, 128), lambda w, k, meta: (2 * (meta[1] ^ k) + (meta[0] ^ w), 0, 0))
    extra = pl.BlockSpec((16, 128), lambda w, k, meta: (late_shards * rows // 16, 0))
    return pl.pallas_call(
        functools.partial(update_kernel, shards, late_shards, shard_rows),
        name="update",
        grid_spec=pltpu.PrefetchScalarGridSpec(
            num_scalar_prefetch=1,
            grid=(2, shards),
            in_specs=[pl.BlockSpec(memory_space=pltpu.SMEM)]
            + [pl.BlockSpec((rows, 128), early_map(side)) for side in range(2)]
            + [pl.BlockSpec((rows, 128), late_map(side)) for side in range(2)]
            + [extra, extra, by_shard, by_half, by_half]
            + [by_half] * (2 * shards),
            out_specs=[pl.BlockSpec(memory_space=ANY), by_half, by_half, by_half],
            scratch_shapes=[
                VECTOR((rows, 128), jnp.float32),
                VECTOR((shards * shard_rows + 2 * rows, 128), jnp.float32),
                VECTOR((2, shards * shard_rows // 9, 128), jnp.bfloat16),
                pltpu.SemaphoreType.DMA((2,)),
            ],
        ),
        out_shape=[jax.ShapeDtypeStruct((shards * shard_rows, 128), jnp.bfloat16)]
        + [jax.ShapeDtypeStruct((shard_rows, 128), jnp.float32)] * 3,
        compiler_params=pltpu.CompilerParams(vmem_limit_bytes=60 * 2**20),
        cost_estimate=BRIEF,
    )(
        meta,
        jnp.stack([1.0 / norm, norm]),
        *early,
        *late,
        *late,
        weights,
        first_moment.reshape(-1, 128),
        second_moment.reshape(-1, 128),
        *moments,
    )


def narrow_kernel(shard_rows, turn_ref, one_ref, two_ref, first_out, second_out):
    shape = first_out.shape
    begin = pl.program_id(0) * shape[0]
    inside = begin + lax.broadcasted_iota(jnp.int32, shape, 0) < shard_rows
    one = jnp.where(inside, one_ref[...], 0.0).astype(jnp.bfloat16)
    two = jnp.where(inside, two_ref[...], 0.0).astype(jnp.bfloat16)
    turned = turn_ref[0] == 1
    first_out[...] = jnp.where(turned, two, one)
    second_out[...] = jnp.where(turned, one, two)


def narrowed(one, two, half, turn):
    block = pl.BlockSpec((half // 2, 128), lambda i: (i, 0))
    return pl.pallas_call(
        functools.partial(narrow_kernel, one.shape[0]),
        name="narrow",
        grid=(4,),
        in_specs=[pl.BlockSpec(memory_space=pltpu.SMEM), block, block],
        out_specs=[block, block],
        out_shape=[jax.ShapeDtypeStruct((2 * half, 128), jnp.bfloat16)] * 2,
        cost_estimate=BRIEF,
    )(turn.reshape(1), one, two)


def bit_of(bit):
    return (lax.axis_index(LINE) // bit) % 2


def on_device(inputs, weights, cotangent, clip_lengths, first_moment, second_moment):
    tok_rows = inputs.shape[0]
    reach = (MOST + tok_rows - 2) // tok_rows
    shard_rows = first_moment.shape[0] // 128
    half = halves_rows(shard_rows)
    (
        first_gain,
        first_bias,
        query_weight,
        query_bias,
        key_weight,
        value_weight,
        value_bias,
        out_weight,
        out_bias,
        second_gain,
        second_bias,
        up_weight,
        up_bias,
        down_weight,
        down_bias,
        padded_weights,
    ) = unpacked(weights, shard_rows)
    base_slot = lax.axis_index(LINE) * tok_rows
    positions = base_slot + jnp.arange(tok_rows, dtype=jnp.int32)
    lower_slot, upper_slot = bounds(positions, clip_lengths)
    low = lower_slot - base_slot + reach * tok_rows
    high = upper_slot - base_slot + reach * tok_rows
    first_block = low.reshape(-1, ROWS_AT)[:, 0] // tok_rows
    last_block = (high.reshape(-1, ROWS_AT)[:, -1] + tok_rows - 1) // tok_rows
    ranges = (first_block, last_block, slot_table(), tok_rows)
    low, high = low[:, None], high[:, None]

    inner = lax.axis_size("inner")
    turn = (lax.axis_index(LINE) // inner) % 2
    first_half, second_half = narrowed(first_moment.reshape(-1, 128), second_moment.reshape(-1, 128), half, turn)
    blocks = halo(inputs, (padded_weights,))
    window = jnp.concatenate(blocks, axis=0)
    fetched, window = lax.optimization_barrier((first_half, window))
    window_hat, _ = standard(window.astype(jnp.float32))
    window_normed = (window_hat * first_gain + first_bias).astype(jnp.bfloat16)
    project = jnp.concatenate([query_weight, key_weight, value_weight], axis=1)
    shift = jnp.concatenate([query_bias, jnp.zeros((1, D), jnp.float32), value_bias], axis=1)
    rows = (plain_dot(window_normed, project) + shift).astype(jnp.bfloat16)
    fetched = swapped(fetched, 2)
    input_rows = inputs.astype(jnp.float32)
    first_hat, first_dev = standard(input_rows)
    normed = (first_hat * first_gain + first_bias).astype(jnp.bfloat16)

    attended, lse = attend(
        forward_kernel,
        ranges,
        [
            (rows, ("own", 0)),
            (rows, ("window", 4)),
            (rows, ("window", 8)),
            (low, ("all", 0)),
            (high, ("all", 0)),
        ],
        [jnp.float32, jnp.float32],
        [pltpu.VMEM((2, 2 * reach + 1, ROWS_AT, tok_rows), jnp.float32)],
    )
    attended, lse, fetched = lax.optimization_barrier((attended, lse, fetched))
    held = {0: (first_half, second_half), 2: (fetched, swapped(fetched, inner))}
    bit = 4
    while bit < inner:
        for place in list(held):
            held[place + bit] = tuple(swapped(piece, bit) for piece in held[place])
        bit = 2 * bit
    moments = []
    for place in range(inner):
        if place % 2 == 0:
            moments += held[place]
        else:
            moments += [swapped(piece, 1) for piece in held[place - 1]]
    mixed = attended.astype(jnp.bfloat16)
    middle = input_rows + plain_dot(mixed, out_weight) + out_bias
    second_hat, second_dev = standard(middle)
    hidden_in = (second_hat * second_gain + second_bias).astype(jnp.bfloat16)
    up_rows = plain_dot(hidden_in, up_weight) + up_bias
    cdf_part = 0.5 * (1.0 + lax.erf(up_rows * INV_ROOT_TWO))
    activated = (up_rows * cdf_part).astype(jnp.bfloat16)
    layer_output = (middle + plain_dot(activated, down_weight) + down_bias).astype(jnp.bfloat16)
    grad_out = cotangent.astype(jnp.float32)
    down_bias_grad = jnp.sum(grad_out, axis=0)
    grad_act = back_dot(cotangent, down_weight)
    pdf_part = jnp.exp(-0.5 * up_rows * up_rows) * INV_ROOT_TWO_PI
    grad_up = (grad_act * (cdf_part + up_rows * pdf_part)).astype(jnp.bfloat16)
    up_bias_grad = jnp.sum(grad_up.astype(jnp.float32), axis=0)
    grad_hidden = back_dot(grad_up, up_weight)
    second_gain_grad = jnp.sum(grad_hidden * second_hat, axis=0)
    second_bias_grad = jnp.sum(grad_hidden, axis=0)
    grad_middle = grad_out + norm_back(grad_hidden, second_hat, second_dev, second_gain)
    grad_branch = grad_middle.astype(jnp.bfloat16)
    out_bias_grad = jnp.sum(grad_branch.astype(jnp.float32), axis=0)
    grad_branch, *moments[4:6] = lax.optimization_barrier((grad_branch, *moments[4:6]))
    sent, delta = mixed_grad(grad_branch, out_weight, attended, lse)
    line = lax.axis_size(LINE)
    shards = inner
    late_shards = shards // 4
    groups = bit_groups()

    def rounded(count, unit):
        return -(-count // unit) * unit

    def shard_spans(first, last, base):
        spans = ([], [])
        for shard in range(first, last):
            begin = (shard - first) * shard_rows + base
            spans[0].append((begin, half, half))
            spans[1].append((begin + half, shard_rows - half, half))
        return spans

    def query_step(pairs, after):
        return attend(
            query_kernel,
            ranges,
            [
                (rows, ("own", 0)),
                (rows, ("window", 4)),
                (rows, ("window", 8)),
                (sent, ("own", 0)),
                (lse, ("own", 0)),
                (delta, ("own", 0)),
                (low, ("all", 0)),
                (high, ("all", 0)),
            ],
            [jnp.bfloat16],
            [],
            pairs,
            after,
        )

    def key_step(pairs, after):
        return attend(
            key_kernel,
            ranges,
            [
                (rows, ("own", 4)),
                (rows, ("own", 8)),
                (rows, ("window", 0)),
                (grad_window, ("window", 0)),
                (low, ("all", 0)),
                (high, ("all", 0)),
            ],
            [jnp.bfloat16, jnp.bfloat16],
            [],
            pairs,
            after,
        )

    query_parts = query_step((0, 2), ())
    grad_window = halo(sent, query_parts)
    grad_window = jnp.concatenate(grad_window, axis=0)
    activated, hidden_in, mixed = (behind(array, query_parts) for array in (activated, hidden_in, mixed))
    down_grad = rows_dot(activated, cotangent)
    up_grad = rows_dot(hidden_in, grad_up)
    out_grad = rows_dot(mixed, grad_branch)

    early_rows = [
        out_grad,
        out_bias_grad,
        second_gain_grad,
        second_bias_grad,
        up_grad,
        up_bias_grad,
        down_grad,
        down_bias_grad,
    ]
    early_rows = [section.reshape(-1, section.shape[-1]) for section in early_rows]
    early_half = rounded((shards - late_shards) * half, 8 * line)
    spans = shard_spans(late_shards, shards, 0)
    for span in spans:
        span.append((0, 0, early_half - (shards - late_shards) * half))
    early_keep, early_give = packed_halves(early_rows, D // 128, spans, early_half)
    early_got = swapped(early_give, 1)

    query_parts += query_step((2, 2), (early_give,))
    parts = combine([early_keep, early_got], groups[0], query_parts)
    got = exchanged(parts, groups[0])
    query_low = jnp.concatenate(query_parts, axis=1)
    work = [(1, 1), (2, 1), (3, 1)]
    done = key_step((0, 1), parts[:1])
    key_parts, value_parts = [done[0]], [done[1]]
    held_back = done[:1]
    for at, group in enumerate(groups):
        parts = combine(got, groups[at + 1] if at + 1 < len(groups) else [], held_back)
        if at + 1 < len(groups):
            got = exchanged(parts, groups[at + 1])
        if work:
            done = key_step(work.pop(0), parts[:1])
            key_parts.append(done[0])
            value_parts.append(done[1])
            held_back = done[:1]
    piece = parts[0]
    for at, group in enumerate(groups[::-1]):
        got = exchanged([piece], group)
        if work and at > 0:
            done = key_step(work.pop(0), [piece])
            key_parts.append(done[0])
            value_parts.append(done[1])
            held_back = done[:1]
        piece = stack(got, group, held_back)
    early_other = swapped(piece, 1)
    for pairs in work:
        done = key_step(pairs, [piece])
        key_parts.append(done[0])
        value_parts.append(done[1])
    early = (piece, early_other)
    key_low = jnp.concatenate(key_parts, axis=1)
    value_low = jnp.concatenate(value_parts, axis=1)
    query_grad = rows_dot(normed, query_low)
    query_bias_grad = jnp.sum(query_low.astype(jnp.float32), axis=0)
    key_grad = rows_dot(normed, key_low)
    value_grad = rows_dot(normed, value_low)
    value_bias_grad = jnp.sum(value_low.astype(jnp.float32), axis=0)
    grad_normed = (
        back_dot(query_low, query_weight)
        + back_dot(key_low, key_weight)
        + back_dot(value_low, value_weight)
    )
    first_gain_grad = jnp.sum(grad_normed * first_hat, axis=0)
    first_bias_grad = jnp.sum(grad_normed, axis=0)
    input_grad = (grad_middle + norm_back(grad_normed, first_hat, first_dev, first_gain)).astype(
        jnp.bfloat16
    )

    late_rows = [
        first_gain_grad,
        first_bias_grad,
        query_grad,
        query_bias_grad,
        key_grad,
        value_grad,
        value_bias_grad,
    ]
    late_rows = [section.reshape(-1, section.shape[-1]) for section in late_rows]
    tail = max(1, 1 << (len(groups[0])))
    late_half = rounded(late_shards * half + 16, 16 * tail)
    spans = shard_spans(0, late_shards, 0)
    spare = late_half - late_shards * half
    spans[0].append((late_shards * shard_rows, D // 128, spare))
    spans[1].append((0, 0, spare))
    keep, give = packed_halves(late_rows, 0, spans, late_half)
    parts = combine([keep, swapped(give, 1)], groups[0], ())
    (piece,) = combine(exchanged(parts, groups[0]), [], ())
    for group in groups[1:]:
        (piece,) = combine(exchanged([piece], group), [], ())
    piece = stack(exchanged([piece], groups[0]), groups[0], ())
    late = (piece, swapped(piece, 1))

    def square_sum(pair):
        sums = [jnp.sum(jnp.square(part.astype(jnp.float32))) for part in pair]
        return sums[0] + sums[1]

    grad_norm = jnp.sqrt(square_sum(early) + square_sum(late))
    steps, grad_shard, moment_one, moment_two = updated(
        jnp.maximum(grad_norm, 1.0), early, late, late_shards, padded_weights, first_moment, second_moment, moments
    )
    weight_step = steps.reshape(-1)
    return (
        layer_output,
        input_grad,
        grad_shard.reshape(-1),
        grad_norm,
        moment_one.reshape(-1),
        moment_two.reshape(-1),
        weight_step,
    )


def solution(mesh):
    return jax.shard_map(
        on_device,
        mesh=mesh,
        in_specs=(
            P(("outer", "inner"), None),
            P(),
            P(("outer", "inner"), None),
            P(),
            P("inner"),
            P("inner"),
        ),
        out_specs=(
            P(("outer", "inner"), None),
            P(("outer", "inner"), None),
            P("inner"),
            P(),
            P("inner"),
            P("inner"),
            P(),
        ),
        check_vma=False,
    )
```

profile of v0, /device:TPU:9, one launch (start us, length us, event | category | flops | bytes accessed | tf_op | source)
XLA Modules:
  0.0 480.0 jit_solution(13956485460875557836)
XLA Ops:
  1.4 3.1 collective-permute-start.1
  4.6 3.9 collective-permute-start.2
  8.5 2.8 collective-permute-start.5
  11.4 13.6 %unpack.1 = (f32[1,512]{1,0:T(1,128)}, f32[1,512]{1,0:T(1,128)}, bf16[512,512]{1,0:T(8,128)(2,1)}, f32[1,512]{1,0:T(1,128)}, bf16[512,512]{1,0:T(8,128)(2,1)}, /...) custom-call(bf16[24624,128]{1,0:T(8,128)(2,1)} %bitcast.60), custom_call_target="tpu_custom_call" | custom-call | flops 1000 | bytes 1000 | tf_op jit(solution)/shard_map/unpack/pallas_call | solution.py:405
  27.2 3.2 collective-permute-done.2
  31.8 5.2 %narrow.1 = (bf16[6272,128]{1,0:T(8,128)(2,1)}, bf16[6272,128]{1,0:T(8,128)(2,1)}) custom-call(s32[1]{0:T(128)} %bitcast.2.turn_ref, f32[6156,128]{1,0:T(8,128)} %bitcast.56, f32[6156,128]{1,0:T(8,128)} %bitcast.58), custom_call_target="tpu_custom_call" | custom-call | flops 1000 | bytes 1000 | tf_op jit(solution)/shard_map/narrow/pallas_call | solution.py:723
  44.6 2.7 convert_reduce_fusion
  47.7 2.3 fusion.2
  50.1 9.2 %add_convert_fusion.q_ref.k_ref.v_ref = bf16[3584,1536]{1,0:T(8,128)(2,1)} fusion(f32[1536]{0:T(1024)S(1)} %fusion.43, bf16[3584,512]{1,0:T(8,128)(2,1)S(1)} %copy-done.8, f32[512]{0:T(512)S(1)} %bitcast.91, f32[512]{0:T(512)S(1)} %bitcast.75, f32[3584]{0:T(1024)S(1)} %add_rsqrt_fusion, f32[3584]{0:T(1024)S(1)} %broadcast_multiply_fusion, ...), kind=kOutput, calls=%fused_computation | convolution fusion | flops 5663883264 | bytes 16291840 | tf_op jit(solution)/shard_map/dot_general | solution.py:46
  59.4 28.1 %shard_map.135 = (f32[512,512]{1,0:T(8,128)S(1)}, f32[512,512]{1,0:T(8,128)S(1)}) custom-call(s32[2]{0:T(128)S(1)} %and_select_fusion.1.first_ref, s32[2]{0:T(128)S(1)} %and_select_fusion.last_ref, s32[7]{0:T(128)S(1)} %broadcast_select_fusion.slot_ref, bf16[3584,1536]{1,0:T(8,128)(2,1)} %add_convert_fusion.q_ref.k_ref.v_ref, ...), custom_call_target="tpu_custom_call" | custom-call | flops 1000 | bytes 1000 | tf_op jit(solution)/shard_map/pallas_call | solution.py:325
  90.7 2.9 multiply_convert_fusion
  93.6 3.3 convert_reduce_fusion.1
  99.0 2.3 convert_reduce_fusion.6
  101.2 15.2 %collective-permute-done.7.refs_5_ = bf16[6272,128]{1,0:T(8,128)(2,1)} collective-permute-done((bf16[6272,128]{1,0:T(8,128)(2,1)S(1)}, bf16[6272,128]{1,0:T(8,128)(2,1)}, u32[]{:S(2)}, u32[]{:S(2)}) %collective-permute-start.7) | collective-permute-done | bytes 1605664 | tf_op jit(solution)/shard_map/ppermute | solution.py:103
  116.4 5.1 %mixed_grad.1 = (bf16[560,512]{1,0:T(8,128)(2,1)}, f32[512,512]{1,0:T(8,128)}) custom-call(bf16[512,512]{1,0:T(8,128)(2,1)} %get-tuple-element.107.branch_ref, bf16[512,512]{1,0:T(8,128)(2,1)} %get-tuple-element.98.weight_ref, f32[512,512]{1,0:T(8,128)} %copy-done.6, f32[512,512]{1,0:T(8,128)} %copy-done), custom_call_target="tpu_custom_call" | custom-call | flops 1000 | bytes 1000 | tf_op jit(solution)/shard_map/mixed_grad/pallas_call | solution.py:292
  123.8 16.0 %shard_map.136 = bf16[512,256]{1,0:T(8,128)(2,1)S(1)} custom-call(s32[2]{0:T(128)S(1)} %and_select_fusion.1.first_ref, s32[2]{0:T(128)S(1)} %and_select_fusion.last_ref, s32[7]{0:T(128)S(1)} %broadcast_select_fusion.slot_ref, bf16[3584,1536]{1,0:T(8,128)(2,1)} %add_convert_fusion.q_ref.k_ref.v_ref, bf16[3584,1536]{1,0:T(8,128)(2,1)} %add_convert_fusion.q_ref.k_ref.v_ref, ...), custom_call_target="tpu_custom_call" | custom-call | flops 1000 | bytes 1000 | tf_op jit(solution)/shard_map/pallas_call | solution.py:325
  141.2 3.3 fusion.55.refs_4_
  144.5 3.3 fusion.56.refs_6_
  147.9 10.6 %pack.2 = (bf16[9472,128]{1,0:T(8,128)(2,1)}, bf16[9472,128]{1,0:T(8,128)(2,1)}) custom-call(s32[1]{0:T(128)} %bitcast.15.place_ref, f32[512,512]{1,0:T(8,128)} %fusion.54.refs_0_, f32[1,512]{1,0:T(1,128)} %bitcast.67, f32[1,512]{1,0:T(1,128)} %bitcast.73, f32[1,512]{1,0:T(1,128)} %bitcast.74, f32[512,2048]{1,0:T(8,128)} %fusion.55.refs_4_, ...), custom_call_target="tpu_custom_call" | custom-call | flops 1000 | bytes 1000 | tf_op jit(solution)/shard_map/pack/pallas_call | solution.py:477
  158.4 14.7 %collective-permute-start.8 = (bf16[9472,128]{1,0:T(8,128)(2,1)}, bf16[9472,128]{1,0:T(8,128)(2,1)}, u32[]{:S(2)}, u32[]{:S(2)}) collective-permute-start(bf16[9472,128]{1,0:T(8,128)(2,1)} %get-tuple-element.114), channel_id=1, source_target_pairs={{1,0},{0,1},{3,2},{2,3},{5,4},{4,5},{7,6},{6,7},{9,8},{8,9},{11,10... | collective-permute-start | bytes 7274504 | tf_op jit(solution)/shard_map/ppermute | solution.py:103
  176.2 11.2 %collective-permute-start.10 = (bf16[560,512]{1,0:T(8,128)(2,1)S(1)}, bf16[560,512]{1,0:T(8,128)(2,1)}, u32[]{:S(2)}, u32[]{:S(2)}) collective-permute-start(bf16[560,512]{1,0:T(8,128)(2,1)S(1)} %copy-done.3), channel_id=1, source_target_pairs={{0,2},{1,3},{2,4},{3,5},{4,6},{5,7},{6,8},{7,9},{8,10},{9,11},{10,... | collective-permute-start | bytes 1720328 | tf_op jit(solution)/shard_map/ppermute | solution.py:98
  190.7 15.8 %shard_map.137 = bf16[512,256]{1,0:T(8,128)(2,1)S(1)} custom-call(s32[2]{0:T(128)S(1)} %and_select_fusion.1.first_ref, s32[2]{0:T(128)S(1)} %and_select_fusion.last_ref, s32[7]{0:T(128)S(1)} %broadcast_select_fusion.slot_ref, bf16[3584,1536]{1,0:T(8,128)(2,1)} %add_convert_fusion.q_ref.k_ref.v_ref, bf16[3584,1536]{1,0:T(8,128)(2,1)} %add_convert_fusion.q_ref.k_ref.v_ref, ...), custom_call_target="tpu_custom_call" | custom-call | flops 1000 | bytes 1000 | tf_op jit(solution)/shard_map/pallas_call | solution.py:325
  208.2 3.4 collective-permute-done.10
  214.5 4.1 collective-permute-start.14
  224.0 4.4 combine.6
  229.1 2.5 collective-permute-start.16
  237.5 12.0 %shard_map.138 = (bf16[512,128]{1,0:T(8,128)(2,1)S(1)}, bf16[512,128]{1,0:T(8,128)(2,1)S(1)}) custom-call(s32[2]{0:T(128)S(1)} %and_select_fusion.1.first_ref, s32[2]{0:T(128)S(1)} %and_select_fusion.last_ref, s32[7]{0:T(128)S(1)} %broadcast_select_fusion.slot_ref, bf16[3584,1536]{1,0:T(8,128)(2,1)} %add_convert_fusion.q_ref.k_ref.v_ref, ...), custom_call_target="tpu_custom_call" | custom-call | flops 1000 | bytes 1000 | tf_op jit(solution)/shard_map/pallas_call | solution.py:325
  249.6 10.1 %collective-permute-done.17.refs_3_ = bf16[2368,128]{1,0:T(8,128)(2,1)} collective-permute-done((bf16[2368,128]{1,0:T(8,128)(2,1)}, bf16[2368,128]{1,0:T(8,128)(2,1)}, u32[]{:S(2)}, u32[]{:S(2)}) %collective-permute-start.17) | collective-permute-done | bytes 606240 | tf_op jit(solution)/shard_map/ppermute | solution.py:103
  259.7 2.7 combine.7
  262.4 11.8 %shard_map.139 = (bf16[512,128]{1,0:T(8,128)(2,1)S(1)}, bf16[512,128]{1,0:T(8,128)(2,1)S(1)}) custom-call(s32[2]{0:T(128)S(1)} %and_select_fusion.1.first_ref, s32[2]{0:T(128)S(1)} %and_select_fusion.last_ref, s32[7]{0:T(128)S(1)} %broadcast_select_fusion.slot_ref, bf16[3584,1536]{1,0:T(8,128)(2,1)} %add_convert_fusion.q_ref.k_ref.v_ref, ...), custom_call_target="tpu_custom_call" | custom-call | flops 1000 | bytes 1000 | tf_op jit(solution)/shard_map/pallas_call | solution.py:325
  274.3 5.3 %collective-permute-start.19 = (bf16[592,128]{1,0:T(8,128)(2,1)S(1)}, bf16[592,128]{1,0:T(8,128)(2,1)S(1)}, u32[]{:S(2)}, u32[]{:S(2)}) collective-permute-start(bf16[592,128]{1,0:T(8,128)(2,1)S(1)} %copy-done.62), channel_id=1, source_target_pairs={{16,0},{17,1},{18,2},{19,3},{20,4},{21,5},{22,6},{23,7},{24,8},{25... | collective-permute-start | bytes 454664 | tf_op jit(solution)/shard_map/ppermute | solution.py:103
  279.7 10.0 %collective-permute-done.19.refs_2_ = bf16[592,128]{1,0:T(8,128)(2,1)S(1)} collective-permute-done((bf16[592,128]{1,0:T(8,128)(2,1)S(1)}, bf16[592,128]{1,0:T(8,128)(2,1)S(1)}, u32[]{:S(2)}, u32[]{:S(2)}) %collective-permute-start.19) | collective-permute-done | bytes 151584 | tf_op jit(solution)/shard_map/ppermute | solution.py:103
  294.4 3.1 collective-permute-start.22
  297.5 11.8 %shard_map.140 = (bf16[512,128]{1,0:T(8,128)(2,1)S(1)}, bf16[512,128]{1,0:T(8,128)(2,1)S(1)}) custom-call(s32[2]{0:T(128)S(1)} %and_select_fusion.1.first_ref, s32[2]{0:T(128)S(1)} %and_select_fusion.last_ref, s32[7]{0:T(128)S(1)} %broadcast_select_fusion.slot_ref, bf16[3584,1536]{1,0:T(8,128)(2,1)} %add_convert_fusion.q_ref.k_ref.v_ref, ...), custom_call_target="tpu_custom_call" | custom-call | flops 1000 | bytes 1000 | tf_op jit(solution)/shard_map/pallas_call | solution.py:325
  313.7 12.0 %shard_map.141 = (bf16[512,128]{1,0:T(8,128)(2,1)S(1)}, bf16[512,128]{1,0:T(8,128)(2,1)S(1)}) custom-call(s32[2]{0:T(128)S(1)} %and_select_fusion.1.first_ref, s32[2]{0:T(128)S(1)} %and_select_fusion.last_ref, s32[7]{0:T(128)S(1)} %broadcast_select_fusion.slot_ref, bf16[3584,1536]{1,0:T(8,128)(2,1)} %add_convert_fusion.q_ref.k_ref.v_ref, ...), custom_call_target="tpu_custom_call" | custom-call | flops 1000 | bytes 1000 | tf_op jit(solution)/shard_map/pallas_call | solution.py:325
  332.5 4.0 pack.3
  336.6 8.6 %collective-permute-start.28 = (bf16[3200,128]{1,0:T(8,128)(2,1)}, bf16[3200,128]{1,0:T(8,128)(2,1)S(1)}, u32[]{:S(2)}, u32[]{:S(2)}) collective-permute-start(bf16[3200,128]{1,0:T(8,128)(2,1)} %get-tuple-element.145), channel_id=1, source_target_pairs={{1,0},{0,1},{3,2},{2,3},{5,4},{4,5},{7,6},{6,7},{9,8},{8,9},{11,10... | collective-permute-start | bytes 2457608 | tf_op jit(solution)/shard_map/ppermute | solution.py:103
  348.8 2.4 combine.9
  352.9 24.9 %collective-permute-done.29.refs_1_ = bf16[800,128]{1,0:T(8,128)(2,1)S(1)} collective-permute-done((bf16[800,128]{1,0:T(8,128)(2,1)}, bf16[800,128]{1,0:T(8,128)(2,1)S(1)}, u32[]{:S(2)}, u32[]{:S(2)}) %collective-permute-start.29) | collective-permute-done | bytes 204832 | tf_op jit(solution)/shard_map/ppermute | solution.py:103
  379.2 5.4 %collective-permute-done.31.refs_3_ = bf16[800,128]{1,0:T(8,128)(2,1)S(1)} collective-permute-done((bf16[800,128]{1,0:T(8,128)(2,1)}, bf16[800,128]{1,0:T(8,128)(2,1)S(1)}, u32[]{:S(2)}, u32[]{:S(2)}) %collective-permute-start.31) | collective-permute-done | bytes 204832 | tf_op jit(solution)/shard_map/ppermute | solution.py:103
  389.9 3.2 stack.26.early_own
  393.2 2.6 collective-permute-start.27
  396.0 11.5 %collective-permute-done.34.refs_3_ = bf16[800,128]{1,0:T(8,128)(2,1)S(1)} collective-permute-done((bf16[800,128]{1,0:T(8,128)(2,1)}, bf16[800,128]{1,0:T(8,128)(2,1)S(1)}, u32[]{:S(2)}, u32[]{:S(2)}) %collective-permute-start.34) | collective-permute-done | bytes 204832 | tf_op jit(solution)/shard_map/ppermute | solution.py:103
  415.9 4.3 collective-permute-done.37.refs_3_
  423.1 3.2 collective-permute-start.38
  427.5 4.4 fusion.24
  439.1 3.1 multiply_reduce_fusion
  444.3 34.4 %update.1 = (bf16[24624,128]{1,0:T(8,128)(2,1)}, f32[6156,128]{1,0:T(8,128)}, f32[6156,128]{1,0:T(8,128)}, f32[6156,128]{1,0:T(8,128)}) custom-call(s32[3]{0:T(128)} %pad_add_fusion.meta_ref, f32[2]{0:T(128)} %pad_maximum_fusion.3.scale_ref, bf16[9472,128]{1,0:T(8,128)(2,1)} %stack.26.early_own, bf16[9472,128]{1,0:T(8,128)(2,1)} %collective-permute-done.27.early_other, ...), custom_call_target="tpu_custom_call" | custom-call | flops 1000 | bytes 1000 | tf_op jit(solution)/shard_map/update/pallas_call | solution.py:674
  (278 shorter events, 91.3 us)
Async XLA Ops:
  0.7 30.3 %copy-start.12 = (bf16[512,512]{1,0:T(8,128)(2,1)S(1)}, bf16[512,512]{1,0:T(8,128)(2,1)}, u32[]{:S(2)}) copy-start(bf16[512,512]{1,0:T(8,128)(2,1)} %param.8) | copy-start | bytes 1572868
  0.7 36.8 %collective-permute-start = (bf16[512,512]{1,0:T(8,128)(2,1)}, bf16[512,512]{1,0:T(8,128)(2,1)S(1)}, u32[]{:S(2)}, u32[]{:S(2)}) collective-permute-start(bf16[512,512]{1,0:T(8,128)(2,1)} %param.8), channel_id=1, source_target_pairs={{1,0},{0,1},{3,2},{2,3},{5,4},{4,5},{7,6},{6,7},{9,8},{8,9},{11,10... | collective-permute-start | bytes 1572872 | tf_op jit(solution)/shard_map/ppermute | solution.py:103
  1.4 25.8 %collective-permute-start.1 = (bf16[512,512]{1,0:T(8,128)(2,1)}, bf16[512,512]{1,0:T(8,128)(2,1)S(1)}, u32[]{:S(2)}, u32[]{:S(2)}) collective-permute-start(bf16[512,512]{1,0:T(8,128)(2,1)} %param.8), channel_id=1, source_target_pairs={{0,2},{1,3},{2,4},{3,5},{4,6},{5,7},{6,8},{7,9},{8,10},{9,11},{10,... | collective-permute-start | bytes 1572872 | tf_op jit(solution)/shard_map/ppermute | solution.py:98
  4.6 25.8 %collective-permute-start.2 = (bf16[512,512]{1,0:T(8,128)(2,1)}, bf16[512,512]{1,0:T(8,128)(2,1)S(1)}, u32[]{:S(2)}, u32[]{:S(2)}) collective-permute-start(bf16[512,512]{1,0:T(8,128)(2,1)} %param.8), channel_id=1, source_target_pairs={{2,0},{3,1},{4,2},{5,3},{6,4},{7,5},{8,6},{9,7},{10,8},{11,9},{12,... | collective-permute-start | bytes 1572872 | tf_op jit(solution)/shard_map/ppermute | solution.py:98
  8.5 35.2 %collective-permute-start.5 = (bf16[512,512]{1,0:T(8,128)(2,1)}, bf16[512,512]{1,0:T(8,128)(2,1)S(1)}, u32[]{:S(2)}, u32[]{:S(2)}) collective-permute-start(bf16[512,512]{1,0:T(8,128)(2,1)} %param.8), channel_id=1, source_target_pairs={{4,1},{6,3},{1,4},{8,5},{3,6},{10,7},{5,8},{12,9},{7,10},{14,11},{... | collective-permute-start | bytes 1572872 | tf_op jit(solution)/shard_map/ppermute | solution.py:112
  30.4 9.5 %collective-permute-start.3 = (bf16[512,512]{1,0:T(8,128)(2,1)S(1)}, bf16[512,512]{1,0:T(8,128)(2,1)}, u32[]{:S(2)}, u32[]{:S(2)}) collective-permute-start(bf16[512,512]{1,0:T(8,128)(2,1)S(1)} %collective-permute-done.1), channel_id=1, source_target_pairs={{1,0},{0,1},{3,2},{2,3},{5,4},{4,5},{7,6},{6,7},{9,8},{8,9},{11,10... | collective-permute-start | bytes 1572872 | tf_op jit(solution)/shard_map/ppermute | solution.py:103
  30.9 10.9 %collective-permute-start.4 = (bf16[512,512]{1,0:T(8,128)(2,1)S(1)}, bf16[512,512]{1,0:T(8,128)(2,1)}, u32[]{:S(2)}, u32[]{:S(2)}) collective-permute-start(bf16[512,512]{1,0:T(8,128)(2,1)S(1)} %collective-permute-done.2), channel_id=1, source_target_pairs={{1,0},{0,1},{3,2},{2,3},{5,4},{4,5},{7,6},{6,7},{9,8},{8,9},{11,10... | collective-permute-start | bytes 1572872 | tf_op jit(solution)/shard_map/ppermute | solution.py:103
  50.0 37.5 %collective-permute-start.6 = (bf16[6272,128]{1,0:T(8,128)(2,1)S(1)}, bf16[6272,128]{1,0:T(8,128)(2,1)S(1)}, u32[]{:S(2)}, u32[]{:S(2)}) collective-permute-start(bf16[6272,128]{1,0:T(8,128)(2,1)S(1)} %copy-done.24), channel_id=1, source_target_pairs={{2,0},{3,1},{0,2},{1,3},{6,4},{7,5},{4,6},{5,7},{10,8},{11,9},{8,1... | collective-permute-start | bytes 4816904 | tf_op jit(solution)/shard_map/ppermute | solution.py:103
  88.4 28.0 %collective-permute-start.7 = (bf16[6272,128]{1,0:T(8,128)(2,1)S(1)}, bf16[6272,128]{1,0:T(8,128)(2,1)}, u32[]{:S(2)}, u32[]{:S(2)}) collective-permute-start(bf16[6272,128]{1,0:T(8,128)(2,1)S(1)} %collective-permute-done.6.refs_4_), channel_id=1, source_target_pairs={{4,0},{5,1},{6,2},{7,3},{0,4},{1,5},{2,6},{3,7},{12,8},{13,9},{14,... | collective-permute-start | bytes 4816904 | tf_op jit(solution)/shard_map/ppermute | solution.py:103
  147.9 28.3 %copy-start.3 = (bf16[560,512]{1,0:T(8,128)(2,1)S(1)}, bf16[560,512]{1,0:T(8,128)(2,1)}, u32[]{:S(2)}) copy-start(bf16[560,512]{1,0:T(8,128)(2,1)} %get-tuple-element.109.g_ref) | copy-start | bytes 1720324
  147.9 42.9 %copy-start.5 = (f32[512,512]{1,0:T(8,128)S(1)}, f32[512,512]{1,0:T(8,128)}, u32[]{:S(2)}) copy-start(f32[512,512]{1,0:T(8,128)} %get-tuple-element.110.delta_ref) | copy-start | bytes 3145732
  158.4 65.5 %collective-permute-start.8 = (bf16[9472,128]{1,0:T(8,128)(2,1)}, bf16[9472,128]{1,0:T(8,128)(2,1)}, u32[]{:S(2)}, u32[]{:S(2)}) collective-permute-start(bf16[9472,128]{1,0:T(8,128)(2,1)} %get-tuple-element.114), channel_id=1, source_target_pairs={{1,0},{0,1},{3,2},{2,3},{5,4},{4,5},{7,6},{6,7},{9,8},{8,9},{11,10... | collective-permute-start | bytes 7274504 | tf_op jit(solution)/shard_map/ppermute | solution.py:103
  176.2 35.4 %collective-permute-start.10 = (bf16[560,512]{1,0:T(8,128)(2,1)S(1)}, bf16[560,512]{1,0:T(8,128)(2,1)}, u32[]{:S(2)}, u32[]{:S(2)}) collective-permute-start(bf16[560,512]{1,0:T(8,128)(2,1)S(1)} %copy-done.3), channel_id=1, source_target_pairs={{0,2},{1,3},{2,4},{3,5},{4,6},{5,7},{6,8},{7,9},{8,10},{9,11},{10,... | collective-permute-start | bytes 1720328 | tf_op jit(solution)/shard_map/ppermute | solution.py:98
  187.4 24.2 %collective-permute-start.11 = (bf16[560,512]{1,0:T(8,128)(2,1)S(1)}, bf16[560,512]{1,0:T(8,128)(2,1)}, u32[]{:S(2)}, u32[]{:S(2)}) collective-permute-start(bf16[560,512]{1,0:T(8,128)(2,1)S(1)} %copy-done.3), channel_id=1, source_target_pairs={{2,0},{3,1},{4,2},{5,3},{6,4},{7,5},{8,6},{9,7},{10,8},{11,9},{12,... | collective-permute-start | bytes 1720328 | tf_op jit(solution)/shard_map/ppermute | solution.py:98
  189.9 29.4 %collective-permute-start.9 = (bf16[560,512]{1,0:T(8,128)(2,1)S(1)}, bf16[560,512]{1,0:T(8,128)(2,1)S(1)}, u32[]{:S(2)}, u32[]{:S(2)}) collective-permute-start(bf16[560,512]{1,0:T(8,128)(2,1)S(1)} %copy-done.3), channel_id=1, source_target_pairs={{1,0},{0,1},{3,2},{2,3},{5,4},{4,5},{7,6},{6,7},{9,8},{8,9},{11,10... | collective-permute-start | bytes 1720328 | tf_op jit(solution)/shard_map/ppermute | solution.py:103
  211.6 20.1 %collective-permute-start.12 = (bf16[560,512]{1,0:T(8,128)(2,1)}, bf16[560,512]{1,0:T(8,128)(2,1)}, u32[]{:S(2)}, u32[]{:S(2)}) collective-permute-start(bf16[560,512]{1,0:T(8,128)(2,1)} %collective-permute-done.10), channel_id=1, source_target_pairs={{1,0},{0,1},{3,2},{2,3},{5,4},{4,5},{7,6},{6,7},{9,8},{8,9},{11,10... | collective-permute-start | bytes 1720328 | tf_op jit(solution)/shard_map/ppermute | solution.py:103
  213.6 21.2 %collective-permute-start.13 = (bf16[560,512]{1,0:T(8,128)(2,1)}, bf16[560,512]{1,0:T(8,128)(2,1)}, u32[]{:S(2)}, u32[]{:S(2)}) collective-permute-start(bf16[560,512]{1,0:T(8,128)(2,1)} %collective-permute-done.11), channel_id=1, source_target_pairs={{1,0},{0,1},{3,2},{2,3},{5,4},{4,5},{7,6},{6,7},{9,8},{8,9},{11,10... | collective-permute-start | bytes 1720328 | tf_op jit(solution)/shard_map/ppermute | solution.py:103
  214.5 22.1 %collective-permute-start.14 = (bf16[560,512]{1,0:T(8,128)(2,1)S(1)}, bf16[560,512]{1,0:T(8,128)(2,1)S(1)}, u32[]{:S(2)}, u32[]{:S(2)}) collective-permute-start(bf16[560,512]{1,0:T(8,128)(2,1)S(1)} %copy-done.3), channel_id=1, source_target_pairs={{4,1},{6,3},{1,4},{8,5},{3,6},{10,7},{5,8},{12,9},{7,10},{14,11},{... | collective-permute-start | bytes 1720328 | tf_op jit(solution)/shard_map/ppermute | solution.py:112
  228.3 21.2 %collective-permute-start.15 = (bf16[2368,128]{1,0:T(8,128)(2,1)}, bf16[2368,128]{1,0:T(8,128)(2,1)}, u32[]{:S(2)}, u32[]{:S(2)}) collective-permute-start(bf16[2368,128]{1,0:T(8,128)(2,1)} %get-tuple-element.124), channel_id=1, source_target_pairs={{2,0},{3,1},{0,2},{1,3},{6,4},{7,5},{4,6},{5,7},{10,8},{11,9},{8,1... | collective-permute-start | bytes 1818632 | tf_op jit(solution)/shard_map/ppermute | solution.py:103
  229.1 20.4 %collective-permute-start.16 = (bf16[2368,128]{1,0:T(8,128)(2,1)}, bf16[2368,128]{1,0:T(8,128)(2,1)}, u32[]{:S(2)}, u32[]{:S(2)}) collective-permute-start(bf16[2368,128]{1,0:T(8,128)(2,1)} %get-tuple-element.125), channel_id=1, source_target_pairs={{4,0},{5,1},{6,2},{7,3},{0,4},{1,5},{2,6},{3,7},{12,8},{13,9},{14,... | collective-permute-start | bytes 1818632 | tf_op jit(solution)/shard_map/ppermute | solution.py:103
  231.7 28.0 %collective-permute-start.17 = (bf16[2368,128]{1,0:T(8,128)(2,1)}, bf16[2368,128]{1,0:T(8,128)(2,1)}, u32[]{:S(2)}, u32[]{:S(2)}) collective-permute-start(bf16[2368,128]{1,0:T(8,128)(2,1)} %get-tuple-element.126), channel_id=1, source_target_pairs={{6,0},{7,1},{4,2},{5,3},{2,4},{3,5},{0,6},{1,7},{14,8},{15,9},{12,... | collective-permute-start | bytes 1818632 | tf_op jit(solution)/shard_map/ppermute | solution.py:103
  274.2 5.4 %collective-permute-start.18 = (bf16[592,128]{1,0:T(8,128)(2,1)S(1)}, bf16[592,128]{1,0:T(8,128)(2,1)S(1)}, u32[]{:S(2)}, u32[]{:S(2)}) collective-permute-start(bf16[592,128]{1,0:T(8,128)(2,1)S(1)} %copy-done.63), channel_id=1, source_target_pairs={{8,0},{9,1},{10,2},{11,3},{12,4},{13,5},{14,6},{15,7},{0,8},{1,9},... | collective-permute-start | bytes 454664 | tf_op jit(solution)/shard_map/ppermute | solution.py:103
  274.3 15.4 %collective-permute-start.19 = (bf16[592,128]{1,0:T(8,128)(2,1)S(1)}, bf16[592,128]{1,0:T(8,128)(2,1)S(1)}, u32[]{:S(2)}, u32[]{:S(2)}) collective-permute-start(bf16[592,128]{1,0:T(8,128)(2,1)S(1)} %copy-done.62), channel_id=1, source_target_pairs={{16,0},{17,1},{18,2},{19,3},{20,4},{21,5},{22,6},{23,7},{24,8},{25... | collective-permute-start | bytes 454664 | tf_op jit(solution)/shard_map/ppermute | solution.py:103
  279.6 12.3 %collective-permute-start.20 = (bf16[592,128]{1,0:T(8,128)(2,1)S(1)}, bf16[592,128]{1,0:T(8,128)(2,1)S(1)}, u32[]{:S(2)}, u32[]{:S(2)}) collective-permute-start(bf16[592,128]{1,0:T(8,128)(2,1)S(1)} %copy-done.61), channel_id=1, source_target_pairs={{24,0},{25,1},{26,2},{27,3},{28,4},{29,5},{30,6},{31,7},{16,8},{17... | collective-permute-start | bytes 454664 | tf_op jit(solution)/shard_map/ppermute | solution.py:103
  294.4 15.0 %collective-permute-start.21 = (bf16[592,128]{1,0:T(8,128)(2,1)}, bf16[592,128]{1,0:T(8,128)(2,1)S(1)}, u32[]{:S(2)}, u32[]{:S(2)}) collective-permute-start(bf16[592,128]{1,0:T(8,128)(2,1)} %combine.8.refs_0_), channel_id=1, source_target_pairs={{8,0},{9,1},{10,2},{11,3},{12,4},{13,5},{14,6},{15,7},{0,8},{1,9},... | collective-permute-start | bytes 454664 | tf_op jit(solution)/shard_map/ppermute | solution.py:103
  294.4 15.0 %collective-permute-start.22 = (bf16[592,128]{1,0:T(8,128)(2,1)}, bf16[592,128]{1,0:T(8,128)(2,1)S(1)}, u32[]{:S(2)}, u32[]{:S(2)}) collective-permute-start(bf16[592,128]{1,0:T(8,128)(2,1)} %combine.8.refs_0_), channel_id=1, source_target_pairs={{16,0},{17,1},{18,2},{19,3},{20,4},{21,5},{22,6},{23,7},{24,8},{25... | collective-permute-start | bytes 454664 | tf_op jit(solution)/shard_map/ppermute | solution.py:103
  297.5 13.5 %collective-permute-start.23 = (bf16[592,128]{1,0:T(8,128)(2,1)}, bf16[592,128]{1,0:T(8,128)(2,1)S(1)}, u32[]{:S(2)}, u32[]{:S(2)}) collective-permute-start(bf16[592,128]{1,0:T(8,128)(2,1)} %combine.8.refs_0_), channel_id=1, source_target_pairs={{24,0},{25,1},{26,2},{27,3},{28,4},{29,5},{30,6},{31,7},{16,8},{17... | collective-permute-start | bytes 454664 | tf_op jit(solution)/shard_map/ppermute | solution.py:103
  336.6 11.3 %collective-permute-start.28 = (bf16[3200,128]{1,0:T(8,128)(2,1)}, bf16[3200,128]{1,0:T(8,128)(2,1)S(1)}, u32[]{:S(2)}, u32[]{:S(2)}) collective-permute-start(bf16[3200,128]{1,0:T(8,128)(2,1)} %get-tuple-element.145), channel_id=1, source_target_pairs={{1,0},{0,1},{3,2},{2,3},{5,4},{4,5},{7,6},{6,7},{9,8},{8,9},{11,10... | collective-permute-start | bytes 2457608 | tf_op jit(solution)/shard_map/ppermute | solution.py:103
  345.2 42.5 %collective-permute-start.24 = (bf16[2368,128]{1,0:T(8,128)(2,1)S(1)}, bf16[2368,128]{1,0:T(8,128)(2,1)S(1)}, u32[]{:S(2)}, u32[]{:S(2)}) collective-permute-start(bf16[2368,128]{1,0:T(8,128)(2,1)S(1)} %copy-done.19), channel_id=1, source_target_pairs={{2,0},{3,1},{0,2},{1,3},{6,4},{7,5},{4,6},{5,7},{10,8},{11,9},{8,1... | collective-permute-start | bytes 1818632 | tf_op jit(solution)/shard_map/ppermute | solution.py:103
  345.2 44.7 %collective-permute-start.25 = (bf16[2368,128]{1,0:T(8,128)(2,1)S(1)}, bf16[2368,128]{1,0:T(8,128)(2,1)}, u32[]{:S(2)}, u32[]{:S(2)}) collective-permute-start(bf16[2368,128]{1,0:T(8,128)(2,1)S(1)} %copy-done.19), channel_id=1, source_target_pairs={{4,0},{5,1},{6,2},{7,3},{0,4},{1,5},{2,6},{3,7},{12,8},{13,9},{14,... | collective-permute-start | bytes 1818632 | tf_op jit(solution)/shard_map/ppermute | solution.py:103
  346.9 43.0 %collective-permute-start.26 = (bf16[2368,128]{1,0:T(8,128)(2,1)S(1)}, bf16[2368,128]{1,0:T(8,128)(2,1)}, u32[]{:S(2)}, u32[]{:S(2)}) collective-permute-start(bf16[2368,128]{1,0:T(8,128)(2,1)S(1)} %copy-done.19), channel_id=1, source_target_pairs={{6,0},{7,1},{4,2},{5,3},{2,4},{3,5},{0,6},{1,7},{14,8},{15,9},{12,... | collective-permute-start | bytes 1818632 | tf_op jit(solution)/shard_map/ppermute | solution.py:103
  351.2 26.6 %collective-permute-start.29 = (bf16[800,128]{1,0:T(8,128)(2,1)}, bf16[800,128]{1,0:T(8,128)(2,1)S(1)}, u32[]{:S(2)}, u32[]{:S(2)}) collective-permute-start(bf16[800,128]{1,0:T(8,128)(2,1)} %get-tuple-element.147), channel_id=1, source_target_pairs={{2,0},{3,1},{0,2},{1,3},{6,4},{7,5},{4,6},{5,7},{10,8},{11,9},{8,1... | collective-permute-start | bytes 614408 | tf_op jit(solution)/shard_map/ppermute | solution.py:103
  351.4 27.8 %collective-permute-start.30 = (bf16[800,128]{1,0:T(8,128)(2,1)}, bf16[800,128]{1,0:T(8,128)(2,1)S(1)}, u32[]{:S(2)}, u32[]{:S(2)}) collective-permute-start(bf16[800,128]{1,0:T(8,128)(2,1)} %get-tuple-element.148), channel_id=1, source_target_pairs={{4,0},{5,1},{6,2},{7,3},{0,4},{1,5},{2,6},{3,7},{12,8},{13,9},{14,... | collective-permute-start | bytes 614408 | tf_op jit(solution)/shard_map/ppermute | solution.py:103
  377.7 6.8 %collective-permute-start.31 = (bf16[800,128]{1,0:T(8,128)(2,1)}, bf16[800,128]{1,0:T(8,128)(2,1)S(1)}, u32[]{:S(2)}, u32[]{:S(2)}) collective-permute-start(bf16[800,128]{1,0:T(8,128)(2,1)} %get-tuple-element.149), channel_id=1, source_target_pairs={{6,0},{7,1},{4,2},{5,3},{2,4},{3,5},{0,6},{1,7},{14,8},{15,9},{12,... | collective-permute-start | bytes 614408 | tf_op jit(solution)/shard_map/ppermute | solution.py:103
  387.2 40.2 %copy-start.10 = (f32[512,512]{1,0:T(8,128)S(1)}, f32[512,512]{1,0:T(8,128)}, u32[]{:S(2)}) copy-start(f32[512,512]{1,0:T(8,128)} %copy-done.9) | copy-start | bytes 3145732
  387.2 40.2 %copy-start.65 = (f32[1,512]{1,0:T(1,128)S(1)}, f32[1,512]{1,0:T(1,128)}, u32[]{:S(2)}) copy-start(f32[1,512]{1,0:T(1,128)} %get-tuple-element.105) | copy-start | bytes 6148
  387.3 8.6 %collective-permute-start.32 = (bf16[800,128]{1,0:T(8,128)(2,1)}, bf16[800,128]{1,0:T(8,128)(2,1)S(1)}, u32[]{:S(2)}, u32[]{:S(2)}) collective-permute-start(bf16[800,128]{1,0:T(8,128)(2,1)} %combine.10.refs_0_), channel_id=1, source_target_pairs={{8,0},{9,1},{10,2},{11,3},{12,4},{13,5},{14,6},{15,7},{0,8},{1,9},... | collective-permute-start | bytes 614408 | tf_op jit(solution)/shard_map/ppermute | solution.py:103
  387.3 8.8 %collective-permute-start.33 = (bf16[800,128]{1,0:T(8,128)(2,1)}, bf16[800,128]{1,0:T(8,128)(2,1)S(1)}, u32[]{:S(2)}, u32[]{:S(2)}) collective-permute-start(bf16[800,128]{1,0:T(8,128)(2,1)} %combine.10.refs_0_), channel_id=1, source_target_pairs={{16,0},{17,1},{18,2},{19,3},{20,4},{21,5},{22,6},{23,7},{24,8},{25... | collective-permute-start | bytes 614408 | tf_op jit(solution)/shard_map/ppermute | solution.py:103
  387.7 19.8 %collective-permute-start.34 = (bf16[800,128]{1,0:T(8,128)(2,1)}, bf16[800,128]{1,0:T(8,128)(2,1)S(1)}, u32[]{:S(2)}, u32[]{:S(2)}) collective-permute-start(bf16[800,128]{1,0:T(8,128)(2,1)} %combine.10.refs_0_), channel_id=1, source_target_pairs={{24,0},{25,1},{26,2},{27,3},{28,4},{29,5},{30,6},{31,7},{16,8},{17... | collective-permute-start | bytes 614408 | tf_op jit(solution)/shard_map/ppermute | solution.py:103
  393.2 45.9 %collective-permute-start.27 = (bf16[9472,128]{1,0:T(8,128)(2,1)}, bf16[9472,128]{1,0:T(8,128)(2,1)}, u32[]{:S(2)}, u32[]{:S(2)}) collective-permute-start(bf16[9472,128]{1,0:T(8,128)(2,1)} %stack.26.early_own), channel_id=1, source_target_pairs={{1,0},{0,1},{3,2},{2,3},{5,4},{4,5},{7,6},{6,7},{9,8},{8,9},{11,10... | collective-permute-start | bytes 7274504 | tf_op jit(solution)/shard_map/ppermute | solution.py:103
  410.2 4.8 %collective-permute-start.35 = (bf16[800,128]{1,0:T(8,128)(2,1)}, bf16[800,128]{1,0:T(8,128)(2,1)S(1)}, u32[]{:S(2)}, u32[]{:S(2)}) collective-permute-start(bf16[800,128]{1,0:T(8,128)(2,1)} %combine.11.refs_0_), channel_id=1, source_target_pairs={{2,0},{3,1},{0,2},{1,3},{6,4},{7,5},{4,6},{5,7},{10,8},{11,9},{8,1... | collective-permute-start | bytes 614408 | tf_op jit(solution)/shard_map/ppermute | solution.py:103
  410.8 5.1 %collective-permute-start.36 = (bf16[800,128]{1,0:T(8,128)(2,1)}, bf16[800,128]{1,0:T(8,128)(2,1)S(1)}, u32[]{:S(2)}, u32[]{:S(2)}) collective-permute-start(bf16[800,128]{1,0:T(8,128)(2,1)} %combine.11.refs_0_), channel_id=1, source_target_pairs={{4,0},{5,1},{6,2},{7,3},{0,4},{1,5},{2,6},{3,7},{12,8},{13,9},{14,... | collective-permute-start | bytes 614408 | tf_op jit(solution)/shard_map/ppermute | solution.py:103
  411.9 8.4 %collective-permute-start.37 = (bf16[800,128]{1,0:T(8,128)(2,1)}, bf16[800,128]{1,0:T(8,128)(2,1)S(1)}, u32[]{:S(2)}, u32[]{:S(2)}) collective-permute-start(bf16[800,128]{1,0:T(8,128)(2,1)} %combine.11.refs_0_), channel_id=1, source_target_pairs={{6,0},{7,1},{4,2},{5,3},{2,4},{3,5},{0,6},{1,7},{14,8},{15,9},{12,... | collective-permute-start | bytes 614408 | tf_op jit(solution)/shard_map/ppermute | solution.py:103
  423.1 8.8 %collective-permute-start.38 = (bf16[3200,128]{1,0:T(8,128)(2,1)}, bf16[3200,128]{1,0:T(8,128)(2,1)S(1)}, u32[]{:S(2)}, u32[]{:S(2)}) collective-permute-start(bf16[3200,128]{1,0:T(8,128)(2,1)} %stack.27.late_own.extra_own), channel_id=1, source_target_pairs={{1,0},{0,1},{3,2},{2,3},{5,4},{4,5},{7,6},{6,7},{9,8},{8,9},{11,10... | collective-permute-start | bytes 2457608 | tf_op jit(solution)/shard_map/ppermute | solution.py:103
  426.4 17.9 %collective-permute-start.39 = (bf16[6272,128]{1,0:T(8,128)(2,1)}, bf16[6272,128]{1,0:T(8,128)(2,1)}, u32[]{:S(2)}, u32[]{:S(2)}) collective-permute-start(bf16[6272,128]{1,0:T(8,128)(2,1)} %get-tuple-element.96.refs_0_), channel_id=1, source_target_pairs={{1,0},{0,1},{3,2},{2,3},{5,4},{4,5},{7,6},{6,7},{9,8},{8,9},{11,10... | collective-permute-start | bytes 4816904 | tf_op jit(solution)/shard_map/ppermute | solution.py:103
  426.4 17.9 %collective-permute-start.40 = (bf16[6272,128]{1,0:T(8,128)(2,1)}, bf16[6272,128]{1,0:T(8,128)(2,1)}, u32[]{:S(2)}, u32[]{:S(2)}) collective-permute-start(bf16[6272,128]{1,0:T(8,128)(2,1)} %get-tuple-element.150.refs_1_), channel_id=1, source_target_pairs={{1,0},{0,1},{3,2},{2,3},{5,4},{4,5},{7,6},{6,7},{9,8},{8,9},{11,10... | collective-permute-start | bytes 4816904 | tf_op jit(solution)/shard_map/ppermute | solution.py:103
  427.4 16.8 %collective-permute-start.41 = (bf16[6272,128]{1,0:T(8,128)(2,1)}, bf16[6272,128]{1,0:T(8,128)(2,1)}, u32[]{:S(2)}, u32[]{:S(2)}) collective-permute-start(bf16[6272,128]{1,0:T(8,128)(2,1)} %copy-done.25), channel_id=1, source_target_pairs={{1,0},{0,1},{3,2},{2,3},{5,4},{4,5},{7,6},{6,7},{9,8},{8,9},{11,10... | collective-permute-start | bytes 4816904 | tf_op jit(solution)/shard_map/ppermute | solution.py:103
  431.9 12.4 %collective-permute-start.42 = (bf16[6272,128]{1,0:T(8,128)(2,1)}, bf16[6272,128]{1,0:T(8,128)(2,1)}, u32[]{:S(2)}, u32[]{:S(2)}) collective-permute-start(bf16[6272,128]{1,0:T(8,128)(2,1)} %collective-permute-done.7.refs_5_), channel_id=1, source_target_pairs={{1,0},{0,1},{3,2},{2,3},{5,4},{4,5},{7,6},{6,7},{9,8},{8,9},{11,10... | collective-permute-start | bytes 4816904 | tf_op jit(solution)/shard_map/ppermute | solution.py:103
  (62 other events, 496.6 us)
where the time goes:
time: 489 us; the launch traced here: 480 us
  Pallas kernels  203 us (42%)
  waiting for transfers between devices  96.6 us (20%)
  starting transfers between devices  85.8 us (18%)
  matrix products  38.6 us (8%)
  local copies, waits for them, and re-layouts  27.3 us (6%)
  other arithmetic  23 us (5%)
  between operations  5.58 us (1%)
    pallas_call x7, Pallas kernels, attend(): pl.pallas_call(functools.partial(kernel, ROWS_AT), grid_spec=pltpu.Prefet...  107 us
    ppermute x37, waiting for transfers between devices, swapped(): return lax.ppermute(block, LINE, [(i ^ bit, i) for i in range(n)])  88.5 us
    ppermute x37, starting transfers between devices, swapped(): return lax.ppermute(block, LINE, [(i ^ bit, i) for i in range(n)])  58.7 us
    pallas_call x1, Pallas kernels, updated(): pl.pallas_call(functools.partial(update_kernel, shards, late_shards, shar...  34.4 us
    unnamed x152, local copies, waits for them, and re-layouts  25.2 us
    ppermute x4, starting transfers between devices, shifted(): lax.ppermute(block, LINE, [(i + distance, i) for i in range(n) if 0 <= i...  20.2 us
    dot_general x4, matrix products, plain_dot(): return jnp.dot(matrix_one, matrix_two, preferred_element_type=jnp.float32)  17.1 us
    pallas_call x6, Pallas kernels, combine(): pl.pallas_call(functools.partial(combine_kernel, len(parts)), name='combi...  15.4 us
  transfers between devices with their start and end apart: 43, of which 15 were waited for; matrix products, arithmetic and copies ran while one was open for 12% of the time, Pallas kernels for 21%

commit v1 on v0

--- a/solution.py
+++ b/solution.py
@@ -9,6 +9,7 @@
 from jax.sharding import PartitionSpec as P
 
 D = 512
+HEADS = 8
 FF = 2048
 MOST = 1500
 
@@ -115,6 +116,13 @@
     return [block, partner, left, right, *turned, far]
 
 
+def block_distances():
+    odd = lax.axis_index(LINE) % 2
+    even_far = jnp.array([0, 1, -2, 2, -1, 3, -3], jnp.int32)
+    odd_far = jnp.array([0, -1, -2, 2, -3, 1, 3], jnp.int32)
+    return jnp.where(odd == 1, odd_far, even_far)
+
+
 def slot_table():
     odd = lax.axis_index(LINE) % 2
     even_slots = jnp.array([6, 2, 4, 0, 1, 3, 5], jnp.int32)
@@ -140,172 +148,247 @@
     return parts[0]
 
 
-def tile_mask(block, shape, low, high):
-    place = block * shape[1] + lax.broadcasted_iota(jnp.int32, shape, 1)
-    return (place >= low) & (place < high)
-
-
-def forward_kernel(rows_at, first_ref, last_ref, slot_ref, q_ref, k_ref, v_ref, low_ref, high_ref, o_ref, lse_ref, s_ref):
-    width = q_ref.shape[0]
-    for i in range(width // rows_at):
-        rows = pl.ds(i * rows_at, rows_at)
-        queries = head_halves(q_ref[rows, :] * jnp.bfloat16(0.125))
-        low, high = low_ref[rows, :], high_ref[rows, :]
-
-        def scores(block, peaks):
-            keys = k_ref[pl.ds(pl.multiple_of(slot_ref[block] * width, width), width), :]
-            mask = tile_mask(block, (rows_at, width), low, high)
-            found = []
-            for h in range(2):
-                score = jnp.where(mask, dot_nt(queries[h], keys), NEG)
-                s_ref[h, block] = score
-                found.append(jnp.maximum(peaks[h], over_lanes(score, jnp.maximum)))
-            return tuple(found)
-
-        start = jnp.full((rows_at, 128), NEG, jnp.float32)
-        peaks = lax.fori_loop(first_ref[i], last_ref[i], scores, (start, start))
-        peaks = [jnp.max(peak, axis=1, keepdims=True) for peak in peaks]
-
-        def mix(block, carried):
-            values = v_ref[pl.ds(pl.multiple_of(slot_ref[block] * width, width), width), :]
-            totals, sums = [], []
-            for h in range(2):
-                soft = jnp.exp(s_ref[h, block] - peaks[h])
-                totals.append(carried[0][h] + over_lanes(soft, jnp.add))
-                sums.append(carried[1][h] + jnp.dot(soft.astype(jnp.bfloat16), values, preferred_element_type=jnp.float32))
-            return tuple(totals), tuple(sums)
-
-        zero = jnp.zeros((rows_at, 128), jnp.float32)
-        totals, sums = lax.fori_loop(first_ref[i], last_ref[i], mix, ((zero, zero), (zero, zero)))
-        totals = [jnp.sum(total, axis=1, keepdims=True) for total in totals]
-        even = lax.broadcasted_iota(jnp.int32, (rows_at, 128), 1) < 64
-        o_ref[rows, :] = jnp.where(even, sums[0] / totals[0], sums[1] / totals[1])
-        lse_ref[rows, :] = jnp.where(even, peaks[0] + jnp.log(totals[0]), peaks[1] + jnp.log(totals[1]))
-
-
-def query_kernel(
-    rows_at, first_ref, last_ref, slot_ref, q_ref, k_ref, v_ref, g_ref, lse_ref, delta_ref, low_ref, high_ref, dq_ref
+LSE_PARTS, DELTA_PARTS = 3, 2
+DELTA_AT = LSE_PARTS * HEADS
+CLIPS_AT = DELTA_AT + DELTA_PARTS * HEADS
+
+
+def lane_of(shape):
+    return lax.broadcasted_iota(jnp.int32, shape, 1)
+
+
+def among(lane, begin, count):
+    return (lane >= begin) & (lane < begin + count)
+
+
+def beside(pair, marks):
+    return jnp.concatenate([pair, marks.astype(pair.dtype)], axis=1)
+
+
+def clip_marks(positions, clip_lengths):
+    ends = jnp.cumsum(clip_lengths, dtype=jnp.int32)
+    starts = ends - clip_lengths
+    spare = 128 - CLIPS_AT - clip_lengths.shape[0]
+    assert spare >= 0
+    big = jnp.iinfo(jnp.int32).max
+    lower = jnp.concatenate([jnp.full((CLIPS_AT,), -big, jnp.int32), starts, jnp.full((spare,), big, jnp.int32)])
+    upper = jnp.concatenate([jnp.full((CLIPS_AT,), big, jnp.int32), ends, jnp.full((spare,), big, jnp.int32)])
+    inside = (positions[:, None] >= lower[None]) & (positions[:, None] < upper[None])
+    return inside.astype(jnp.bfloat16)
+
+
+def penalty(marks):
+    closed = (lane_of(marks.shape) >= CLIPS_AT) & (marks == 0)
+    return jnp.where(closed, NEG, 0.0).astype(jnp.bfloat16)
+
+
+def forward_kernel(
+    begin, rows_at, first_ref, last_ref, slot_ref, q_ref, k_ref, v_ref, mark_ref, closed_ref, o_ref, lse_ref, s_ref
 ):
     width = q_ref.shape[0]
     for i in range(width // rows_at):
         rows = pl.ds(i * rows_at, rows_at)
-        queries = head_halves(q_ref[rows, :] * jnp.bfloat16(0.125))
-        grads = head_halves(g_ref[rows, :])
-        low, high = low_ref[rows, :], high_ref[rows, :]
-        lse = [lse_ref[rows, 64 * h : 64 * h + 1] for h in range(2)]
-        delta = [delta_ref[rows, 64 * h : 64 * h + 1] for h in range(2)]
+        queries = [
+            beside(half, closed_ref[rows, :]) for half in head_halves(q_ref[rows, :] * jnp.bfloat16(0.125))
+        ]
+
+        def scores(block, peaks):
+            at = pl.ds(pl.multiple_of(slot_ref[block] * width, width), width)
+            keys = beside(k_ref[at, :], mark_ref[at, :])
+            found = []
+            for h in range(2):
+                score = dot_nt(queries[h], keys)
+                s_ref[h, block] = score
+                found.append(jnp.maximum(peaks[h], over_lanes(score, jnp.maximum)))
+            return tuple(found)
+
+        start = jnp.full((rows_at, 128), NEG, jnp.float32)
+        peaks = lax.fori_loop(first_ref[i], last_ref[i], scores, (start, start))
+        peaks = [jnp.max(peak, axis=1, keepdims=True) for peak in peaks]
+
+        def mix(block, sums):
+            at = pl.ds(pl.multiple_of(slot_ref[block] * width, width), width)
+            values = beside(v_ref[at, :], mark_ref[at, :])
+            found = []
+            for h in range(2):
+                soft = jnp.exp(s_ref[h, block] - peaks[h]).astype(jnp.bfloat16)
+                found.append(sums[h] + jnp.dot(soft, values, preferred_element_type=jnp.float32))
+            return tuple(found)
+
+        zero = jnp.zeros((rows_at, 256), jnp.float32)
+        sums = lax.fori_loop(first_ref[i], last_ref[i], mix, (zero, zero))
+        totals = [part[:, 128:129] for part in sums]
+        even = lane_of((rows_at, 128)) < 64
+        o_ref[rows, :] = jnp.where(even, sums[0][:, :128] / totals[0], sums[1][:, :128] / totals[1])
+        lse_ref[rows, :] = jnp.where(even, peaks[0] + jnp.log(totals[0]), peaks[1] + jnp.log(totals[1]))
+
+
+def query_kernel(
+    begin, rows_at, first_ref, last_ref, slot_ref, q_ref, k_ref, v_ref, g_ref, own_ref, mark_ref, closed_ref, dq_ref
+):
+    width = q_ref.shape[0]
+    pair = pl.program_id(0) + begin
+    for i in range(width // rows_at):
+        rows = pl.ds(i * rows_at, rows_at)
+        own, closed = own_ref[rows, :], closed_ref[rows, :]
+        lane = lane_of(own.shape)
+        zero = jnp.zeros_like(own)
+        queries, grads = [], []
+        halves = zip(head_halves(q_ref[rows, :] * jnp.bfloat16(0.125)), head_halves(g_ref[rows, :]))
+        for h, (query, grad) in enumerate(halves):
+            head = 2 * pair + h
+            queries.append(beside(query, jnp.where(among(lane, LSE_PARTS * head, LSE_PARTS), own, closed)))
+            grads.append(beside(grad, jnp.where(among(lane, DELTA_AT + DELTA_PARTS * head, DELTA_PARTS), own, zero)))
 
         def step(block, carried):
             at = pl.ds(pl.multiple_of(slot_ref[block] * width, width), width)
-            keys, values = k_ref[at, :], v_ref[at, :]
-            mask = tile_mask(block, (rows_at, width), low, high)
+            keys = k_ref[at, :]
+            values = beside(v_ref[at, :], mark_ref[at, :])
+            marked = beside(keys, mark_ref[at, :])
             found = []
             for h in range(2):
-                soft = jnp.exp(jnp.where(mask, dot_nt(queries[h], keys) - lse[h], NEG))
-                grad = (soft * (dot_nt(grads[h], values) - delta[h])).astype(jnp.bfloat16)
+                soft = jnp.exp(dot_nt(queries[h], marked))
+                grad = (soft * dot_nt(grads[h], values)).astype(jnp.bfloat16)
                 found.append(carried[h] + jnp.dot(grad, keys, preferred_element_type=jnp.float32))
             return tuple(found)
 
-        zero = jnp.zeros((rows_at, 128), jnp.float32)
-        sums = lax.fori_loop(first_ref[i], last_ref[i], step, (zero, zero))
-        even = lax.broadcasted_iota(jnp.int32, (rows_at, 128), 1) < 64
-        dq_ref[rows, :] = (jnp.where(even, sums[0], sums[1]) * 0.125).astype(jnp.bfloat16)
-
-
-def key_kernel(
-    rows_at, first_ref, last_ref, slot_ref, k_ref, v_ref, q_ref, g_ref, low_ref, high_ref, dk_ref, dv_ref
-):
+        start = jnp.zeros((rows_at, 128), jnp.float32)
+        sums = lax.fori_loop(first_ref[i], last_ref[i], step, (start, start))
+        dq_ref[rows, :] = (jnp.where(lane < 64, sums[0], sums[1]) * 0.125).astype(jnp.bfloat16)
+
+
+def key_kernel(begin, rows_at, first_ref, last_ref, slot_ref, k_ref, v_ref, q_ref, closed_ref, *refs):
+    dk_ref, dv_ref, grad_ref, mark_ref = refs[-4:]
     width = k_ref.shape[0]
-    sent = width + stat_rows(width)
+    pair = pl.program_id(0) + begin
+    blocks = grad_ref.shape[0]
+    for j in range(blocks):
+        grad_ref[j] = refs[j][...]
+
+    @pl.when(pl.program_id(0) == 0)
+    def _():
+        for j in range(blocks):
+            mark_ref[j] = refs[blocks + j][...]
+
     for i in range(width // rows_at):
         rows = pl.ds(i * rows_at, rows_at)
-        keys = head_halves(k_ref[rows, :] * jnp.bfloat16(0.125))
-        values = head_halves(v_ref[rows, :])
-        low, high = low_ref[rows, :], high_ref[rows, :]
+        closed = closed_ref[rows, :]
+        lane = lane_of(closed.shape)
+        one, zero = jnp.ones_like(closed), jnp.zeros_like(closed)
+        keys, values = [], []
+        halves = zip(head_halves(k_ref[rows, :] * jnp.bfloat16(0.125)), head_halves(v_ref[rows, :]))
+        for h, (key, value) in enumerate(halves):
+            head = 2 * pair + h
+            keys.append(beside(key, jnp.where(among(lane, LSE_PARTS * head, LSE_PARTS), one, closed)))
+            values.append(beside(value, jnp.where(among(lane, DELTA_AT + DELTA_PARTS * head, DELTA_PARTS), one, zero)))
 
         def step(block, carried):
             slot = slot_ref[block]
-            at = pl.ds(pl.multiple_of(slot * width, width), width)
-            queries = q_ref[at, :]
-            grads = g_ref[pl.ds(pl.multiple_of(slot * sent, 16), width), :]
-            packed = g_ref[pl.ds(pl.multiple_of(slot * sent + width, 16), sent - width), :].astype(jnp.float32)
-            mask = tile_mask(block, (rows_at, width), low, high)
+            queries = q_ref[pl.ds(pl.multiple_of(slot * width, width), width), :]
+            grads, marks = grad_ref[slot], mark_ref[slot]
+            marked, graded = beside(queries, marks), beside(grads, marks)
             key_sums, value_sums = [], []
             for h in range(2):
-                lse = unpacked_stat(packed, h, width)
-                delta = unpacked_stat(packed, 2 + h, width)
-                soft = jnp.exp(jnp.where(mask, dot_nt(keys[h], queries) - lse, NEG))
+                soft = jnp.exp(dot_nt(keys[h], marked))
                 value_sums.append(
                     carried[1][h] + jnp.dot(soft.astype(jnp.bfloat16), grads, preferred_element_type=jnp.float32)
                 )
-                grad = (soft * (dot_nt(values[h], grads) - delta)).astype(jnp.bfloat16)
+                grad = (soft * dot_nt(values[h], graded)).astype(jnp.bfloat16)
                 key_sums.append(carried[0][h] + jnp.dot(grad, queries, preferred_element_type=jnp.float32))
             return tuple(key_sums), tuple(value_sums)
 
-        zero = jnp.zeros((rows_at, 128), jnp.float32)
-        key_sums, value_sums = lax.fori_loop(first_ref[i], last_ref[i], step, ((zero, zero), (zero, zero)))
-        even = lax.broadcasted_iota(jnp.int32, (rows_at, 128), 1) < 64
-        dk_ref[rows, :] = (jnp.where(even, key_sums[0], key_sums[1]) * 0.125).astype(jnp.bfloat16)
-        dv_ref[rows, :] = jnp.where(even, value_sums[0], value_sums[1]).astype(jnp.bfloat16)
-
-
-def stat_rows(width):
-    return -(-12 * (width // 128) // 16) * 16
-
-
-def unpacked_stat(packed, which, width):
-    pieces = width // 128
-    parts = []
-    for j in range(pieces):
-        at = [(3 * which + part) * pieces + j for part in range(3)]
-        parts.append(packed[at[0] : at[0] + 1] + packed[at[1] : at[1] + 1] + packed[at[2] : at[2] + 1])
-    return jnp.concatenate(parts, axis=1)
-
-
-def mixed_grad_kernel(branch_ref, weight_ref, mixed_ref, lse_ref, sent_ref, delta_ref):
-    width = branch_ref.shape[0]
-    grad = dot_nt(branch_ref[...], weight_ref[...]).astype(jnp.bfloat16)
-    sent_ref[pl.ds(0, width), :] = grad
-    product = grad.astype(jnp.float32) * mixed_ref[...]
-    even = lax.broadcasted_iota(jnp.int32, product.shape, 1) < 64
-    sums = [jnp.sum(part, axis=1, keepdims=True) for part in head_halves(product)]
-    delta = jnp.where(even, sums[0], sums[1])
-    delta_ref[...] = delta
-    rows = []
-    for kept in (lse_ref[...], delta):
-        turned = kept.T
-        for h in range(2):
-            row = turned[64 * h : 64 * h + 1, :]
-            for _ in range(3):
-                part = row.astype(jnp.bfloat16).astype(jnp.float32)
-                row = row - part
-                rows.extend(part[:, 128 * j : 128 * (j + 1)] for j in range(width // 128))
-    spare = stat_rows(width) - len(rows)
-    if spare:
-        rows.append(jnp.zeros((spare, 128), jnp.float32))
-    sent_ref[pl.ds(width, stat_rows(width)), :] = jnp.concatenate(rows, axis=0).astype(jnp.bfloat16)
-
-
-def mixed_grad(branch, out_weight, mixed, lse):
+        start = jnp.zeros((rows_at, 128), jnp.float32)
+        key_sums, value_sums = lax.fori_loop(first_ref[i], last_ref[i], step, ((start, start), (start, start)))
+        dk_ref[rows, :] = (jnp.where(lane < 64, key_sums[0], key_sums[1]) * 0.125).astype(jnp.bfloat16)
+        dv_ref[rows, :] = jnp.where(lane < 64, value_sums[0], value_sums[1]).astype(jnp.bfloat16)
+
+
+def mixed_grad_kernel(branch_ref, weight_ref, mixed_ref, lse_ref, own_ref, sent_ref, mark_ref):
+    step = pl.program_id(0)
+
+    @pl.when(step == 0)
+    def _():
+        mark_ref[...] = own_ref[...].astype(jnp.float32)
+
+    @pl.when(step < D // 128)
+    def _():
+        grad = dot_nt(branch_ref[...], weight_ref[...]).astype(jnp.bfloat16)
+        sent_ref[...] = grad
+        product = grad.astype(jnp.float32) * mixed_ref[...]
+        lane = lane_of(product.shape)
+        for h, part in enumerate(head_halves(product)):
+            head = 2 * step + h
+            delta = -jnp.sum(part, axis=1, keepdims=True)
+            lse = -lse_ref[:, 64 * h : 64 * h + 1]
+            for value, begin, count in (
+                (lse, LSE_PARTS * head, LSE_PARTS),
+                (delta, DELTA_AT + DELTA_PARTS * head, DELTA_PARTS),
+            ):
+                for k in range(count):
+                    rounded = value.astype(jnp.bfloat16).astype(jnp.float32)
+                    mark_ref[...] = jnp.where(lane == begin + k, rounded, mark_ref[...])
+                    value = value - rounded
+
+    @pl.when(step == D // 128)
+    def _():
+        sent_ref[...] = mark_ref[...].astype(jnp.bfloat16)
+
+
+def mixed_grad(branch, out_weight, mixed, lse, own_marks):
     width = branch.shape[0]
-    column = pl.BlockSpec((width, 128), lambda h: (0, h))
+    last = D // 128 - 1
+    column = pl.BlockSpec((width, 128), lambda h: (0, jnp.minimum(h, last)))
     return pl.pallas_call(
         mixed_grad_kernel,
         name="mixed_grad",
-        grid=(D // 128,),
+        grid=(D // 128 + 1,),
         in_specs=[
             pl.BlockSpec((width, D), lambda h: (0, 0)),
-            pl.BlockSpec((128, D), lambda h: (h, 0)),
+            pl.BlockSpec((128, D), lambda h: (jnp.minimum(h, last), 0)),
             column,
             column,
+            pl.BlockSpec((width, 128), lambda h: (0, 0)),
         ],
-        out_specs=[pl.BlockSpec((width + stat_rows(width), 128), lambda h: (0, h)), column],
-        out_shape=[
-            jax.ShapeDtypeStruct((width + stat_rows(width), D), jnp.bfloat16),
-            jax.ShapeDtypeStruct((width, D), jnp.float32),
-        ],
+        out_specs=pl.BlockSpec((width, 128), lambda h: (0, h)),
+        out_shape=jax.ShapeDtypeStruct((width, D + 128), jnp.bfloat16),
+        scratch_shapes=[pltpu.VMEM((width, 128), jnp.float32)],
         cost_estimate=BRIEF,
-    )(branch, out_weight, mixed, lse)
+    )(branch, out_weight, mixed, lse, own_marks)
+
+
+def project_kernel(count, *refs):
+    query_ref, key_ref, value_ref, gain_ref, bias_ref, query_bias_ref, value_bias_ref, out_ref, row_ref = refs[count:]
+    step = pl.program_id(0)
+    for j in range(count):
+
+        @pl.when(step == j)
+        def _():
+            row_ref[...] = refs[j][...]
+
+    rows = 256
+    for i in range(row_ref.shape[0] // rows):
+        at = pl.ds(i * rows, rows)
+        hat, _ = standard(row_ref[at, :].astype(jnp.float32))
+        normed = (hat * gain_ref[...] + bias_ref[...]).astype(jnp.bfloat16)
+        out_ref[at, 0:D] = (plain_dot(normed, query_ref[...]) + query_bias_ref[...]).astype(jnp.bfloat16)
+        out_ref[at, D : 2 * D] = plain_dot(normed, key_ref[...]).astype(jnp.bfloat16)
+        out_ref[at, 2 * D :] = (plain_dot(normed, value_ref[...]) + value_bias_ref[...]).astype(jnp.bfloat16)
+
+
+def projected(blocks, *weights):
+    width = blocks[0].shape[0]
+    whole = [pl.BlockSpec(array.shape, lambda i: (0, 0)) for array in (*blocks, *weights)]
+    return pl.pallas_call(
+        functools.partial(project_kernel, len(blocks)),
+        name="project",
+        grid=(len(blocks),),
+        in_specs=whole,
+        out_specs=pl.BlockSpec((width, 3 * D), lambda i: (i, 0)),
+        out_shape=jax.ShapeDtypeStruct((len(blocks) * width, 3 * D), jnp.bfloat16),
+        scratch_shapes=[pltpu.VMEM((width, D), jnp.bfloat16)],
+        compiler_params=pltpu.CompilerParams(vmem_limit_bytes=48 * 2**20),
+        cost_estimate=BRIEF,
+    )(*blocks, *weights)
 
 
 ROWS_AT = 256
@@ -313,17 +396,19 @@
 
 def attend(kernel, ranges, operands, results, scratch, pairs=(0, D // 128), after=()):
     begin, count = pairs
+    tok_rows = ranges[3]
     specs = []
     for array, (kind, at) in operands:
-        if kind == "own":
-            specs.append(pl.BlockSpec((ranges[3], 128), lambda h, *_, at=at + begin: (0, at + h)))
-        elif kind == "window":
-            specs.append(pl.BlockSpec((array.shape[0], 128), lambda h, *_, at=at + begin: (0, at + h)))
+        if kind == "pair":
+            rows = array.shape[0] if at < 0 else tok_rows
+            at = (abs(at) - 1 if at < 0 else at) + begin
+            specs.append(pl.BlockSpec((rows, 128), lambda h, *_, at=at: (0, at + h)))
+        elif kind == "column":
+            specs.append(pl.BlockSpec((tok_rows, 128), lambda h, *_, at=at: (0, at)))
         else:
             specs.append(pl.BlockSpec(array.shape, lambda h, *_, n=array.ndim: (0,) * n))
-    tok_rows = ranges[3]
     return pl.pallas_call(
-        functools.partial(kernel, ROWS_AT),
+        functools.partial(kernel, begin, ROWS_AT),
         grid_spec=pltpu.PrefetchScalarGridSpec(
             num_scalar_prefetch=3,
             grid=(count,),
@@ -766,19 +851,18 @@
     first_block = low.reshape(-1, ROWS_AT)[:, 0] // tok_rows
     last_block = (high.reshape(-1, ROWS_AT)[:, -1] + tok_rows - 1) // tok_rows
     ranges = (first_block, last_block, slot_table(), tok_rows)
-    low, high = low[:, None], high[:, None]
+    places = base_slot + block_distances()[:, None] * tok_rows + jnp.arange(tok_rows, dtype=jnp.int32)[None]
+    marks = clip_marks(places.reshape(-1), clip_lengths)
+    closed = penalty(clip_marks(positions, clip_lengths))
 
     inner = lax.axis_size("inner")
     turn = (lax.axis_index(LINE) // inner) % 2
     first_half, second_half = narrowed(first_moment.reshape(-1, 128), second_moment.reshape(-1, 128), half, turn)
     blocks = halo(inputs, (padded_weights,))
-    window = jnp.concatenate(blocks, axis=0)
-    fetched, window = lax.optimization_barrier((first_half, window))
-    window_hat, _ = standard(window.astype(jnp.float32))
-    window_normed = (window_hat * first_gain + first_bias).astype(jnp.bfloat16)
-    project = jnp.concatenate([query_weight, key_weight, value_weight], axis=1)
-    shift = jnp.concatenate([query_bias, jnp.zeros((1, D), jnp.float32), value_bias], axis=1)
-    rows = (plain_dot(window_normed, project) + shift).astype(jnp.bfloat16)
+    fetched, *blocks = lax.optimization_barrier((first_half, *blocks))
+    rows = projected(
+        blocks, query_weight, key_weight, value_weight, first_gain, first_bias, query_bias, value_bias
+    )
     fetched = swapped(fetched, 2)
     input_rows = inputs.astype(jnp.float32)
     first_hat, first_dev = standard(input_rows)
@@ -788,11 +872,11 @@
         forward_kernel,
         ranges,
         [
-            (rows, ("own", 0)),
-            (rows, ("window", 4)),
-            (rows, ("window", 8)),
-            (low, ("all", 0)),
-            (high, ("all", 0)),
+            (rows, ("pair", 0)),
+            (rows, ("pair", -5)),
+            (rows, ("pair", -9)),
+            (marks, ("all", 0)),
+            (closed, ("all", 0)),
         ],
         [jnp.float32, jnp.float32],
         [pltpu.VMEM((2, 2 * reach + 1, ROWS_AT, tok_rows), jnp.float32)],
@@ -831,7 +915,7 @@
     grad_branch = grad_middle.astype(jnp.bfloat16)
     out_bias_grad = jnp.sum(grad_branch.astype(jnp.float32), axis=0)
     grad_branch, *moments[4:6] = lax.optimization_barrier((grad_branch, *moments[4:6]))
-    sent, delta = mixed_grad(grad_branch, out_weight, attended, lse)
+    sent = mixed_grad(grad_branch, out_weight, attended, lse, clip_marks(positions, clip_lengths))
     line = lax.axis_size(LINE)
     shards = inner
     late_shards = shards // 4
@@ -853,14 +937,13 @@
             query_kernel,
             ranges,
             [
-                (rows, ("own", 0)),
-                (rows, ("window", 4)),
-                (rows, ("window", 8)),
-                (sent, ("own", 0)),
-                (lse, ("own", 0)),
-                (delta, ("own", 0)),
-                (low, ("all", 0)),
-                (high, ("all", 0)),
+                (rows, ("pair", 0)),
+                (rows, ("pair", -5)),
+                (rows, ("pair", -9)),
+                (sent, ("pair", 0)),
+                (sent, ("column", 4)),
+                (marks, ("all", 0)),
+                (closed, ("all", 0)),
             ],
             [jnp.bfloat16],
             [],
@@ -873,22 +956,21 @@
             key_kernel,
             ranges,
             [
-                (rows, ("own", 4)),
-                (rows, ("own", 8)),
-                (rows, ("window", 0)),
-                (grad_window, ("window", 0)),
-                (low, ("all", 0)),
-                (high, ("all", 0)),
-            ],
+                (rows, ("pair", 4)),
+                (rows, ("pair", 8)),
+                (rows, ("pair", -1)),
+                (closed, ("all", 0)),
+            ]
+            + [(block, ("pair", 0)) for block in grad_blocks]
+            + [(block, ("column", 4)) for block in grad_blocks],
             [jnp.bfloat16, jnp.bfloat16],
-            [],
+            [pltpu.VMEM((len(grad_blocks), tok_rows, 128), jnp.bfloat16)] * 2,
             pairs,
             after,
         )
 
     query_parts = query_step((0, 2), ())
-    grad_window = halo(sent, query_parts)
-    grad_window = jnp.concatenate(grad_window, axis=0)
+    grad_blocks = halo(sent, query_parts)
     activated, hidden_in, mixed = (behind(array, query_parts) for array in (activated, hidden_in, mixed))
     down_grad = rows_dot(activated, cotangent)
     up_grad = rows_dot(hidden_in, grad_up)

time: 489 us -> 482 us (0.986)
  the two profiles are of different devices: /device:TPU:9 before, /device:TPU:18 now
where the time goes in v1:
time: 482 us; the launch traced here: 472 us
  Pallas kernels  244 us (51%)
  waiting for transfers between devices  105 us (22%)
  starting transfers between devices  45 us (9%)
  matrix products  31 us (6%)
  other arithmetic  22.6 us (5%)
  local copies, waits for them, and re-layouts  18.9 us (4%)
  between operations  5.66 us (1%)
    pallas_call x7, Pallas kernels, attend(): pl.pallas_call(functools.partial(kernel, begin, ROWS_AT), grid_spec=pltpu...  136 us
    ppermute x37, waiting for transfers between devices, swapped(): return lax.ppermute(block, LINE, [(i ^ bit, i) for i in range(n)])  83.4 us
    pallas_call x1, Pallas kernels, updated(): pl.pallas_call(functools.partial(update_kernel, shards, late_shards, shar...  34.4 us
    ppermute x37, starting transfers between devices, swapped(): return lax.ppermute(block, LINE, [(i ^ bit, i) for i in range(n)])  25.7 us
    ppermute x4, waiting for transfers between devices, shifted(): lax.ppermute(block, LINE, [(i + distance, i) for i in range(n) if 0 <= i...  21.8 us
    unnamed x148, local copies, waits for them, and re-layouts  18.7 us
    pallas_call x6, Pallas kernels, combine(): pl.pallas_call(functools.partial(combine_kernel, len(parts)), name='combi...  15.3 us
    pallas_call x2, Pallas kernels, packed_halves(): pl.pallas_call(functools.partial(pack_kernel, plan, spans), name='pack',...  14.6 us
  transfers between devices with their start and end apart: 43, of which 13 were waited for; matrix products, arithmetic and copies ran while one was open for 9% of the time, Pallas kernels for 31%

profile of v1, /device:TPU:18, one launch (start us, length us, event | category | flops | bytes accessed | tf_op | source)
XLA Modules:
  0.0 472.3 jit_solution(16429327718059190669)
XLA Ops:
  0.7 3.4 collective-permute-start.1
  4.2 3.3 collective-permute-start.2
  7.5 2.9 collective-permute-start.5
  12.7 13.6 %unpack.1 = (f32[1,512]{1,0:T(1,128)}, f32[1,512]{1,0:T(1,128)}, bf16[512,512]{1,0:T(8,128)(2,1)}, f32[1,512]{1,0:T(1,128)}, bf16[512,512]{1,0:T(8,128)(2,1)}, /...) custom-call(bf16[24624,128]{1,0:T(8,128)(2,1)} %bitcast.66), custom_call_target="tpu_custom_call" | custom-call | flops 1000 | bytes 1000 | tf_op jit(solution)/shard_map/unpack/pallas_call | solution.py:490
  26.5 5.3 %narrow.1 = (bf16[6272,128]{1,0:T(8,128)(2,1)}, bf16[6272,128]{1,0:T(8,128)(2,1)}) custom-call(s32[1]{0:T(128)} %bitcast.2.turn_ref, f32[6156,128]{1,0:T(8,128)} %bitcast.62, f32[6156,128]{1,0:T(8,128)} %bitcast.64), custom_call_target="tpu_custom_call" | custom-call | flops 1000 | bytes 1000 | tf_op jit(solution)/shard_map/narrow/pallas_call | solution.py:808
  43.3 11.4 %project.1.q_ref.k_ref.v_ref = bf16[3584,1536]{1,0:T(8,128)(2,1)} custom-call(bf16[512,512]{1,0:T(8,128)(2,1)S(1)} %copy-done.4, bf16[512,512]{1,0:T(8,128)(2,1)S(1)} %copy-done.20, bf16[512,512]{1,0:T(8,128)(2,1)} %collective-permute-done.1.refs_2_, bf16[512,512]{1,0:T(8,128)(2,1)} %collective-permute-done.2.refs_3_, bf16[512,512]{1,0:T(8,128)(2,1)S(1)} %copy-done.22, ...), custom_call_target="tpu_custom_call" | custom-call | flops 1000 | bytes 1000 | tf_op jit(solution)/shard_map/project/pallas_call | solution.py:381
  54.7 37.4 %shard_map.153 = (f32[512,512]{1,0:T(8,128)S(1)}, f32[512,512]{1,0:T(8,128)S(1)}) custom-call(s32[2]{0:T(128)S(1)} %and_select_fusion.1.first_ref, s32[2]{0:T(128)S(1)} %and_select_fusion.last_ref, s32[7]{0:T(128)S(1)} %get-tuple-element.191.slot_ref, bf16[3584,1536]{1,0:T(8,128)(2,1)} %project.1.q_ref.k_ref.v_ref, ...), custom_call_target="tpu_custom_call" | custom-call | flops 1000 | bytes 1000 | tf_op jit(solution)/shard_map/pallas_call | solution.py:410
  95.3 2.9 multiply_convert_fusion
  98.2 3.2 convert_reduce_fusion
  103.6 2.3 convert_reduce_fusion.5
  105.9 23.5 %collective-permute-done.7.refs_5_ = bf16[6272,128]{1,0:T(8,128)(2,1)} collective-permute-done((bf16[6272,128]{1,0:T(8,128)(2,1)}, bf16[6272,128]{1,0:T(8,128)(2,1)}, u32[]{:S(2)}, u32[]{:S(2)}) %collective-permute-start.7) | collective-permute-done | bytes 1605664 | tf_op jit(solution)/shard_map/ppermute | solution.py:104
  129.4 5.2 %mixed_grad.1.g_ref.own_ref.refs_0_.refs_7_ = bf16[512,640]{1,0:T(8,128)(2,1)} custom-call(bf16[512,512]{1,0:T(8,128)(2,1)} %get-tuple-element.117.branch_ref, bf16[512,512]{1,0:T(8,128)(2,1)} %get-tuple-element.108.weight_ref, f32[512,512]{1,0:T(8,128)} %copy-done.8, f32[512,512]{1,0:T(8,128)} %copy-done.16, bf16[512,128]{1,0:T(8,128)(2,1)} %and_convert_fusion.1.own_ref), custom_call_target="tpu_custom_call" | custom-call | flops 1000 | bytes 1000 | tf_op jit(solution)/shard_map/mixed_grad/pallas_call | solution.py:341
  135.7 20.4 %shard_map.154 = bf16[512,256]{1,0:T(8,128)(2,1)S(1)} custom-call(s32[2]{0:T(128)S(1)} %and_select_fusion.1.first_ref, s32[2]{0:T(128)S(1)} %and_select_fusion.last_ref, s32[7]{0:T(128)S(1)} %get-tuple-element.191.slot_ref, bf16[3584,1536]{1,0:T(8,128)(2,1)} %project.1.q_ref.k_ref.v_ref, bf16[3584,1536]{1,0:T(8,128)(2,1)} %project.1.q_ref.k_ref.v_ref, ...), custom_call_target="tpu_custom_call" | custom-call | flops 1000 | bytes 1000 | tf_op jit(solution)/shard_map/pallas_call | solution.py:410
  158.2 3.3 fusion.38.refs_4_
  161.5 3.3 fusion.39.refs_6_
  164.8 10.5 %pack.2 = (bf16[9472,128]{1,0:T(8,128)(2,1)}, bf16[9472,128]{1,0:T(8,128)(2,1)}) custom-call(s32[1]{0:T(128)} %bitcast.11.place_ref, f32[512,512]{1,0:T(8,128)} %fusion.37.refs_0_, f32[1,512]{1,0:T(1,128)} %bitcast.71, f32[1,512]{1,0:T(1,128)} %bitcast.77, f32[1,512]{1,0:T(1,128)} %bitcast.78, f32[512,2048]{1,0:T(8,128)} %fusion.38.refs_4_, ...), custom_call_target="tpu_custom_call" | custom-call | flops 1000 | bytes 1000 | tf_op jit(solution)/shard_map/pack/pallas_call | solution.py:562
  178.1 4.8 %collective-permute-start.11 = (bf16[512,640]{1,0:T(8,128)(2,1)S(1)}, bf16[512,640]{1,0:T(8,128)(2,1)S(1)}, u32[]{:S(2)}, u32[]{:S(2)}) collective-permute-start(bf16[512,640]{1,0:T(8,128)(2,1)S(1)} %copy-done.1), channel_id=1, source_target_pairs={{2,0},{3,1},{4,2},{5,3},{6,4},{7,5},{8,6},{9,7},{10,8},{11,9},{12,... | collective-permute-start | bytes 1966088 | tf_op jit(solution)/shard_map/ppermute | solution.py:99
  182.9 3.0 collective-permute-start.14
  187.8 17.8 %collective-permute-done.10.refs_2_.refs_9_ = bf16[512,640]{1,0:T(8,128)(2,1)S(1)} collective-permute-done((bf16[512,640]{1,0:T(8,128)(2,1)S(1)}, bf16[512,640]{1,0:T(8,128)(2,1)S(1)}, u32[]{:S(2)}, u32[]{:S(2)}) %collective-permute-start.10) | collective-permute-done | bytes 655392 | tf_op jit(solution)/shard_map/ppermute | solution.py:99
  205.6 4.0 collective-permute-done.11.refs_3_.refs_10_
  211.9 19.9 %shard_map.155 = bf16[512,256]{1,0:T(8,128)(2,1)S(1)} custom-call(s32[2]{0:T(128)S(1)} %and_select_fusion.1.first_ref, s32[2]{0:T(128)S(1)} %and_select_fusion.last_ref, s32[7]{0:T(128)S(1)} %get-tuple-element.191.slot_ref, bf16[3584,1536]{1,0:T(8,128)(2,1)} %project.1.q_ref.k_ref.v_ref, bf16[3584,1536]{1,0:T(8,128)(2,1)} %project.1.q_ref.k_ref.v_ref, ...), custom_call_target="tpu_custom_call" | custom-call | flops 1000 | bytes 1000 | tf_op jit(solution)/shard_map/pallas_call | solution.py:410
  232.5 4.3 combine.6
  237.0 3.4 collective-permute-start.17
  240.4 2.6 fusion.25
  246.4 14.7 %shard_map.156 = (bf16[512,128]{1,0:T(8,128)(2,1)S(1)}, bf16[512,128]{1,0:T(8,128)(2,1)S(1)}) custom-call(s32[2]{0:T(128)S(1)} %and_select_fusion.1.first_ref, s32[2]{0:T(128)S(1)} %and_select_fusion.last_ref, s32[7]{0:T(128)S(1)} %get-tuple-element.191.slot_ref, bf16[3584,1536]{1,0:T(8,128)(2,1)} %project.1.q_ref.k_ref.v_ref, ...), custom_call_target="tpu_custom_call" | custom-call | flops 1000 | bytes 1000 | tf_op jit(solution)/shard_map/pallas_call | solution.py:410
  262.6 4.7 collective-permute-done.17.refs_3_
  267.2 2.7 combine.7
  269.9 3.5 collective-permute-start.20
  273.4 14.5 %shard_map.157 = (bf16[512,128]{1,0:T(8,128)(2,1)S(1)}, bf16[512,128]{1,0:T(8,128)(2,1)S(1)}) custom-call(s32[2]{0:T(128)S(1)} %and_select_fusion.1.first_ref, s32[2]{0:T(128)S(1)} %and_select_fusion.last_ref, s32[7]{0:T(128)S(1)} %get-tuple-element.191.slot_ref, bf16[3584,1536]{1,0:T(8,128)(2,1)} %project.1.q_ref.k_ref.v_ref, ...), custom_call_target="tpu_custom_call" | custom-call | flops 1000 | bytes 1000 | tf_op jit(solution)/shard_map/pallas_call | solution.py:410
  291.2 3.5 collective-permute-start.23
  294.7 14.5 %shard_map.158 = (bf16[512,128]{1,0:T(8,128)(2,1)S(1)}, bf16[512,128]{1,0:T(8,128)(2,1)S(1)}) custom-call(s32[2]{0:T(128)S(1)} %and_select_fusion.1.first_ref, s32[2]{0:T(128)S(1)} %and_select_fusion.last_ref, s32[7]{0:T(128)S(1)} %get-tuple-element.191.slot_ref, bf16[3584,1536]{1,0:T(8,128)(2,1)} %project.1.q_ref.k_ref.v_ref, ...), custom_call_target="tpu_custom_call" | custom-call | flops 1000 | bytes 1000 | tf_op jit(solution)/shard_map/pallas_call | solution.py:410
  312.6 14.8 %shard_map.159 = (bf16[512,128]{1,0:T(8,128)(2,1)S(1)}, bf16[512,128]{1,0:T(8,128)(2,1)S(1)}) custom-call(s32[2]{0:T(128)S(1)} %and_select_fusion.1.first_ref, s32[2]{0:T(128)S(1)} %and_select_fusion.last_ref, s32[7]{0:T(128)S(1)} %get-tuple-element.191.slot_ref, bf16[3584,1536]{1,0:T(8,128)(2,1)} %project.1.q_ref.k_ref.v_ref, ...), custom_call_target="tpu_custom_call" | custom-call | flops 1000 | bytes 1000 | tf_op jit(solution)/shard_map/pallas_call | solution.py:410
  332.0 2.2 fusion.20
  334.2 4.1 pack.3
  338.6 3.4 collective-permute-start.26
  342.9 2.4 combine.9
  345.9 26.0 %collective-permute-done.29.refs_1_ = bf16[800,128]{1,0:T(8,128)(2,1)S(1)} collective-permute-done((bf16[800,128]{1,0:T(8,128)(2,1)}, bf16[800,128]{1,0:T(8,128)(2,1)S(1)}, u32[]{:S(2)}, u32[]{:S(2)}) %collective-permute-start.29) | collective-permute-done | bytes 204832 | tf_op jit(solution)/shard_map/ppermute | solution.py:104
  371.9 7.6 %collective-permute-done.31.refs_3_ = bf16[800,128]{1,0:T(8,128)(2,1)S(1)} collective-permute-done((bf16[800,128]{1,0:T(8,128)(2,1)}, bf16[800,128]{1,0:T(8,128)(2,1)S(1)}, u32[]{:S(2)}, u32[]{:S(2)}) %collective-permute-start.31) | collective-permute-done | bytes 204832 | tf_op jit(solution)/shard_map/ppermute | solution.py:104
  382.6 3.1 collective-permute-start.34
  386.6 3.4 stack.26.early_own
  390.4 6.5 %collective-permute-done.33.refs_2_ = bf16[800,128]{1,0:T(8,128)(2,1)} collective-permute-done((bf16[800,128]{1,0:T(8,128)(2,1)}, bf16[800,128]{1,0:T(8,128)(2,1)}, u32[]{:S(2)}, u32[]{:S(2)}) %collective-permute-start.33) | collective-permute-done | bytes 204832 | tf_op jit(solution)/shard_map/ppermute | solution.py:104
  396.9 5.6 %collective-permute-done.34.refs_3_ = bf16[800,128]{1,0:T(8,128)(2,1)} collective-permute-done((bf16[800,128]{1,0:T(8,128)(2,1)}, bf16[800,128]{1,0:T(8,128)(2,1)}, u32[]{:S(2)}, u32[]{:S(2)}) %collective-permute-start.34) | collective-permute-done | bytes 204832 | tf_op jit(solution)/shard_map/ppermute | solution.py:104
  405.8 2.3 collective-permute-start.37
  408.0 3.8 collective-permute-done.35.refs_1_
  413.7 2.6 collective-permute-done.37.refs_3_
  420.1 3.8 fusion.8
  431.3 3.1 multiply_reduce_fusion
  436.5 34.4 %update.1 = (bf16[24624,128]{1,0:T(8,128)(2,1)}, f32[6156,128]{1,0:T(8,128)}, f32[6156,128]{1,0:T(8,128)}, f32[6156,128]{1,0:T(8,128)}) custom-call(s32[3]{0:T(128)} %pad_add_fusion.2.meta_ref, f32[2]{0:T(128)} %pad_maximum_fusion.3.scale_ref, bf16[9472,128]{1,0:T(8,128)(2,1)} %stack.26.early_own, bf16[9472,128]{1,0:T(8,128)(2,1)} %collective-permute-done.27.early_other, ...), custom_call_target="tpu_custom_call" | custom-call | flops 1000 | bytes 1000 | tf_op jit(solution)/shard_map/update/pallas_call | solution.py:759
  (274 shorter events, 67.5 us)
Async XLA Ops:
  0.6 33.5 %collective-permute-start = (bf16[512,512]{1,0:T(8,128)(2,1)}, bf16[512,512]{1,0:T(8,128)(2,1)S(1)}, u32[]{:S(2)}, u32[]{:S(2)}) collective-permute-start(bf16[512,512]{1,0:T(8,128)(2,1)} %refs_0_), channel_id=1, source_target_pairs={{1,0},{0,1},{3,2},{2,3},{5,4},{4,5},{7,6},{6,7},{9,8},{8,9},{11,10... | collective-permute-start | bytes 1572872 | tf_op jit(solution)/shard_map/ppermute | solution.py:104
  0.7 31.4 %collective-permute-start.1 = (bf16[512,512]{1,0:T(8,128)(2,1)}, bf16[512,512]{1,0:T(8,128)(2,1)}, u32[]{:S(2)}, u32[]{:S(2)}) collective-permute-start(bf16[512,512]{1,0:T(8,128)(2,1)} %refs_0_), channel_id=1, source_target_pairs={{0,2},{1,3},{2,4},{3,5},{4,6},{5,7},{6,8},{7,9},{8,10},{9,11},{10,... | collective-permute-start | bytes 1572872 | tf_op jit(solution)/shard_map/ppermute | solution.py:99
  4.2 28.0 %collective-permute-start.2 = (bf16[512,512]{1,0:T(8,128)(2,1)}, bf16[512,512]{1,0:T(8,128)(2,1)}, u32[]{:S(2)}, u32[]{:S(2)}) collective-permute-start(bf16[512,512]{1,0:T(8,128)(2,1)} %refs_0_), channel_id=1, source_target_pairs={{2,0},{3,1},{4,2},{5,3},{6,4},{7,5},{8,6},{9,7},{10,8},{11,9},{12,... | collective-permute-start | bytes 1572872 | tf_op jit(solution)/shard_map/ppermute | solution.py:99
  7.5 27.4 %collective-permute-start.5 = (bf16[512,512]{1,0:T(8,128)(2,1)}, bf16[512,512]{1,0:T(8,128)(2,1)}, u32[]{:S(2)}, u32[]{:S(2)}) collective-permute-start(bf16[512,512]{1,0:T(8,128)(2,1)} %refs_0_), channel_id=1, source_target_pairs={{4,1},{6,3},{1,4},{8,5},{3,6},{10,7},{5,8},{12,9},{7,10},{14,11},{... | collective-permute-start | bytes 1572872 | tf_op jit(solution)/shard_map/ppermute | solution.py:113
  32.2 3.4 collective-permute-start.3
  33.8 2.5 collective-permute-start.4
  37.2 55.0 %collective-permute-start.6 = (bf16[6272,128]{1,0:T(8,128)(2,1)}, bf16[6272,128]{1,0:T(8,128)(2,1)}, u32[]{:S(2)}, u32[]{:S(2)}) collective-permute-start(bf16[6272,128]{1,0:T(8,128)(2,1)} %get-tuple-element.106.refs_0_), channel_id=1, source_target_pairs={{2,0},{3,1},{0,2},{1,3},{6,4},{7,5},{4,6},{5,7},{10,8},{11,9},{8,1... | collective-permute-start | bytes 4816904 | tf_op jit(solution)/shard_map/ppermute | solution.py:104
  39.9 94.7 %copy-start.2 = (bf16[3584,128]{1,0:T(8,128)(2,1)}, bf16[3584,128]{1,0:T(8,128)(2,1)S(1)}, u32[]{:S(2)}) copy-start(bf16[3584,128]{1,0:T(8,128)(2,1)S(1)} %and_convert_fusion.mark_ref) | copy-start | bytes 2752516
  54.7 37.6 %copy-start.44 = (bf16[512,512]{1,0:T(8,128)(2,1)S(1)}, bf16[512,512]{1,0:T(8,128)(2,1)}, u32[]{:S(2)}) copy-start(bf16[512,512]{1,0:T(8,128)(2,1)} %get-tuple-element.108.weight_ref) | copy-start | bytes 1572868
  54.7 37.6 %copy-start.62 = (f32[1,512]{1,0:T(1,128)S(1)}, f32[1,512]{1,0:T(1,128)}, u32[]{:S(2)}) copy-start(f32[1,512]{1,0:T(1,128)} %get-tuple-element.109) | copy-start | bytes 6148
  93.5 35.9 %collective-permute-start.7 = (bf16[6272,128]{1,0:T(8,128)(2,1)}, bf16[6272,128]{1,0:T(8,128)(2,1)}, u32[]{:S(2)}, u32[]{:S(2)}) collective-permute-start(bf16[6272,128]{1,0:T(8,128)(2,1)} %collective-permute-done.6.refs_4_), channel_id=1, source_target_pairs={{4,0},{5,1},{6,2},{7,3},{0,4},{1,5},{2,6},{3,7},{12,8},{13,9},{14,... | collective-permute-start | bytes 4816904 | tf_op jit(solution)/shard_map/ppermute | solution.py:104
  175.4 57.1 %collective-permute-start.8 = (bf16[9472,128]{1,0:T(8,128)(2,1)}, bf16[9472,128]{1,0:T(8,128)(2,1)}, u32[]{:S(2)}, u32[]{:S(2)}) collective-permute-start(bf16[9472,128]{1,0:T(8,128)(2,1)} %get-tuple-element.122), channel_id=1, source_target_pairs={{1,0},{0,1},{3,2},{2,3},{5,4},{4,5},{7,6},{6,7},{9,8},{8,9},{11,10... | collective-permute-start | bytes 7274504 | tf_op jit(solution)/shard_map/ppermute | solution.py:104
  175.6 61.3 %collective-permute-start.9 = (bf16[512,640]{1,0:T(8,128)(2,1)S(1)}, bf16[512,640]{1,0:T(8,128)(2,1)S(1)}, u32[]{:S(2)}, u32[]{:S(2)}) collective-permute-start(bf16[512,640]{1,0:T(8,128)(2,1)S(1)} %copy-done.1), channel_id=1, source_target_pairs={{1,0},{0,1},{3,2},{2,3},{5,4},{4,5},{7,6},{6,7},{9,8},{8,9},{11,10... | collective-permute-start | bytes 1966088 | tf_op jit(solution)/shard_map/ppermute | solution.py:104
  176.2 29.5 %collective-permute-start.10 = (bf16[512,640]{1,0:T(8,128)(2,1)S(1)}, bf16[512,640]{1,0:T(8,128)(2,1)S(1)}, u32[]{:S(2)}, u32[]{:S(2)}) collective-permute-start(bf16[512,640]{1,0:T(8,128)(2,1)S(1)} %copy-done.1), channel_id=1, source_target_pairs={{0,2},{1,3},{2,4},{3,5},{4,6},{5,7},{6,8},{7,9},{8,10},{9,11},{10,... | collective-permute-start | bytes 1966088 | tf_op jit(solution)/shard_map/ppermute | solution.py:99
  178.1 31.6 %collective-permute-start.11 = (bf16[512,640]{1,0:T(8,128)(2,1)S(1)}, bf16[512,640]{1,0:T(8,128)(2,1)S(1)}, u32[]{:S(2)}, u32[]{:S(2)}) collective-permute-start(bf16[512,640]{1,0:T(8,128)(2,1)S(1)} %copy-done.1), channel_id=1, source_target_pairs={{2,0},{3,1},{4,2},{5,3},{6,4},{7,5},{8,6},{9,7},{10,8},{11,9},{12,... | collective-permute-start | bytes 1966088 | tf_op jit(solution)/shard_map/ppermute | solution.py:99
  182.9 54.1 %collective-permute-start.14 = (bf16[512,640]{1,0:T(8,128)(2,1)S(1)}, bf16[512,640]{1,0:T(8,128)(2,1)S(1)}, u32[]{:S(2)}, u32[]{:S(2)}) collective-permute-start(bf16[512,640]{1,0:T(8,128)(2,1)S(1)} %copy-done.1), channel_id=1, source_target_pairs={{4,1},{6,3},{1,4},{8,5},{3,6},{10,7},{5,8},{12,9},{7,10},{14,11},{... | collective-permute-start | bytes 1966088 | tf_op jit(solution)/shard_map/ppermute | solution.py:113
  209.7 36.8 %collective-permute-start.12 = (bf16[512,640]{1,0:T(8,128)(2,1)S(1)}, bf16[512,640]{1,0:T(8,128)(2,1)}, u32[]{:S(2)}, u32[]{:S(2)}) collective-permute-start(bf16[512,640]{1,0:T(8,128)(2,1)S(1)} %collective-permute-done.10.refs_2_.refs_9_), channel_id=1, source_target_pairs={{1,0},{0,1},{3,2},{2,3},{5,4},{4,5},{7,6},{6,7},{9,8},{8,9},{11,10... | collective-permute-start | bytes 1966088 | tf_op jit(solution)/shard_map/ppermute | solution.py:104
  209.7 36.8 %collective-permute-start.13 = (bf16[512,640]{1,0:T(8,128)(2,1)S(1)}, bf16[512,640]{1,0:T(8,128)(2,1)}, u32[]{:S(2)}, u32[]{:S(2)}) collective-permute-start(bf16[512,640]{1,0:T(8,128)(2,1)S(1)} %collective-permute-done.11.refs_3_.refs_10_), channel_id=1, source_target_pairs={{1,0},{0,1},{3,2},{2,3},{5,4},{4,5},{7,6},{6,7},{9,8},{8,9},{11,10... | collective-permute-start | bytes 1966088 | tf_op jit(solution)/shard_map/ppermute | solution.py:104
  236.8 25.7 %collective-permute-start.15 = (bf16[2368,128]{1,0:T(8,128)(2,1)}, bf16[2368,128]{1,0:T(8,128)(2,1)}, u32[]{:S(2)}, u32[]{:S(2)}) collective-permute-start(bf16[2368,128]{1,0:T(8,128)(2,1)} %get-tuple-element.132), channel_id=1, source_target_pairs={{2,0},{3,1},{0,2},{1,3},{6,4},{7,5},{4,6},{5,7},{10,8},{11,9},{8,1... | collective-permute-start | bytes 1818632 | tf_op jit(solution)/shard_map/ppermute | solution.py:104
  236.9 25.6 %collective-permute-start.16 = (bf16[2368,128]{1,0:T(8,128)(2,1)}, bf16[2368,128]{1,0:T(8,128)(2,1)}, u32[]{:S(2)}, u32[]{:S(2)}) collective-permute-start(bf16[2368,128]{1,0:T(8,128)(2,1)} %get-tuple-element.133), channel_id=1, source_target_pairs={{4,0},{5,1},{6,2},{7,3},{0,4},{1,5},{2,6},{3,7},{12,8},{13,9},{14,... | collective-permute-start | bytes 1818632 | tf_op jit(solution)/shard_map/ppermute | solution.py:104
  237.0 30.2 %collective-permute-start.17 = (bf16[2368,128]{1,0:T(8,128)(2,1)}, bf16[2368,128]{1,0:T(8,128)(2,1)}, u32[]{:S(2)}, u32[]{:S(2)}) collective-permute-start(bf16[2368,128]{1,0:T(8,128)(2,1)} %get-tuple-element.134), channel_id=1, source_target_pairs={{6,0},{7,1},{4,2},{5,3},{2,4},{3,5},{0,6},{1,7},{14,8},{15,9},{12,... | collective-permute-start | bytes 1818632 | tf_op jit(solution)/shard_map/ppermute | solution.py:104
  269.9 19.4 %collective-permute-start.18 = (bf16[592,128]{1,0:T(8,128)(2,1)}, bf16[592,128]{1,0:T(8,128)(2,1)}, u32[]{:S(2)}, u32[]{:S(2)}) collective-permute-start(bf16[592,128]{1,0:T(8,128)(2,1)} %get-tuple-element.139), channel_id=1, source_target_pairs={{8,0},{9,1},{10,2},{11,3},{12,4},{13,5},{14,6},{15,7},{0,8},{1,9},... | collective-permute-start | bytes 454664 | tf_op jit(solution)/shard_map/ppermute | solution.py:104
  269.9 19.4 %collective-permute-start.19 = (bf16[592,128]{1,0:T(8,128)(2,1)}, bf16[592,128]{1,0:T(8,128)(2,1)}, u32[]{:S(2)}, u32[]{:S(2)}) collective-permute-start(bf16[592,128]{1,0:T(8,128)(2,1)} %get-tuple-element.140), channel_id=1, source_target_pairs={{16,0},{17,1},{18,2},{19,3},{20,4},{21,5},{22,6},{23,7},{24,8},{25... | collective-permute-start | bytes 454664 | tf_op jit(solution)/shard_map/ppermute | solution.py:104
  269.9 19.4 %collective-permute-start.20 = (bf16[592,128]{1,0:T(8,128)(2,1)}, bf16[592,128]{1,0:T(8,128)(2,1)}, u32[]{:S(2)}, u32[]{:S(2)}) collective-permute-start(bf16[592,128]{1,0:T(8,128)(2,1)} %get-tuple-element.141), channel_id=1, source_target_pairs={{24,0},{25,1},{26,2},{27,3},{28,4},{29,5},{30,6},{31,7},{16,8},{17... | collective-permute-start | bytes 454664 | tf_op jit(solution)/shard_map/ppermute | solution.py:104
  291.2 19.4 %collective-permute-start.21 = (bf16[592,128]{1,0:T(8,128)(2,1)}, bf16[592,128]{1,0:T(8,128)(2,1)}, u32[]{:S(2)}, u32[]{:S(2)}) collective-permute-start(bf16[592,128]{1,0:T(8,128)(2,1)} %combine.8.refs_0_), channel_id=1, source_target_pairs={{8,0},{9,1},{10,2},{11,3},{12,4},{13,5},{14,6},{15,7},{0,8},{1,9},... | collective-permute-start | bytes 454664 | tf_op jit(solution)/shard_map/ppermute | solution.py:104
  291.2 19.4 %collective-permute-start.22 = (bf16[592,128]{1,0:T(8,128)(2,1)}, bf16[592,128]{1,0:T(8,128)(2,1)}, u32[]{:S(2)}, u32[]{:S(2)}) collective-permute-start(bf16[592,128]{1,0:T(8,128)(2,1)} %combine.8.refs_0_), channel_id=1, source_target_pairs={{16,0},{17,1},{18,2},{19,3},{20,4},{21,5},{22,6},{23,7},{24,8},{25... | collective-permute-start | bytes 454664 | tf_op jit(solution)/shard_map/ppermute | solution.py:104
  291.2 19.4 %collective-permute-start.23 = (bf16[592,128]{1,0:T(8,128)(2,1)}, bf16[592,128]{1,0:T(8,128)(2,1)}, u32[]{:S(2)}, u32[]{:S(2)}) collective-permute-start(bf16[592,128]{1,0:T(8,128)(2,1)} %combine.8.refs_0_), channel_id=1, source_target_pairs={{24,0},{25,1},{26,2},{27,3},{28,4},{29,5},{30,6},{31,7},{16,8},{17... | collective-permute-start | bytes 454664 | tf_op jit(solution)/shard_map/ppermute | solution.py:104
  338.4 3.6 collective-permute-start.28
  338.4 44.2 %collective-permute-start.24 = (bf16[2368,128]{1,0:T(8,128)(2,1)S(1)}, bf16[2368,128]{1,0:T(8,128)(2,1)S(1)}, u32[]{:S(2)}, u32[]{:S(2)}) collective-permute-start(bf16[2368,128]{1,0:T(8,128)(2,1)S(1)} %copy-done.41), channel_id=1, source_target_pairs={{2,0},{3,1},{0,2},{1,3},{6,4},{7,5},{4,6},{5,7},{10,8},{11,9},{8,1... | collective-permute-start | bytes 1818632 | tf_op jit(solution)/shard_map/ppermute | solution.py:104
  338.5 47.2 %collective-permute-start.25 = (bf16[2368,128]{1,0:T(8,128)(2,1)S(1)}, bf16[2368,128]{1,0:T(8,128)(2,1)S(1)}, u32[]{:S(2)}, u32[]{:S(2)}) collective-permute-start(bf16[2368,128]{1,0:T(8,128)(2,1)S(1)} %copy-done.41), channel_id=1, source_target_pairs={{4,0},{5,1},{6,2},{7,3},{0,4},{1,5},{2,6},{3,7},{12,8},{13,9},{14,... | collective-permute-start | bytes 1818632 | tf_op jit(solution)/shard_map/ppermute | solution.py:104
  338.6 48.0 %collective-permute-start.26 = (bf16[2368,128]{1,0:T(8,128)(2,1)S(1)}, bf16[2368,128]{1,0:T(8,128)(2,1)}, u32[]{:S(2)}, u32[]{:S(2)}) collective-permute-start(bf16[2368,128]{1,0:T(8,128)(2,1)S(1)} %copy-done.41), channel_id=1, source_target_pairs={{6,0},{7,1},{4,2},{5,3},{2,4},{3,5},{0,6},{1,7},{14,8},{15,9},{12,... | collective-permute-start | bytes 1818632 | tf_op jit(solution)/shard_map/ppermute | solution.py:104
  345.3 26.6 %collective-permute-start.29 = (bf16[800,128]{1,0:T(8,128)(2,1)}, bf16[800,128]{1,0:T(8,128)(2,1)S(1)}, u32[]{:S(2)}, u32[]{:S(2)}) collective-permute-start(bf16[800,128]{1,0:T(8,128)(2,1)} %get-tuple-element.155), channel_id=1, source_target_pairs={{2,0},{3,1},{0,2},{1,3},{6,4},{7,5},{4,6},{5,7},{10,8},{11,9},{8,1... | collective-permute-start | bytes 614408 | tf_op jit(solution)/shard_map/ppermute | solution.py:104
  345.4 26.6 %collective-permute-start.30 = (bf16[800,128]{1,0:T(8,128)(2,1)}, bf16[800,128]{1,0:T(8,128)(2,1)S(1)}, u32[]{:S(2)}, u32[]{:S(2)}) collective-permute-start(bf16[800,128]{1,0:T(8,128)(2,1)} %get-tuple-element.156), channel_id=1, source_target_pairs={{4,0},{5,1},{6,2},{7,3},{0,4},{1,5},{2,6},{3,7},{12,8},{13,9},{14,... | collective-permute-start | bytes 614408 | tf_op jit(solution)/shard_map/ppermute | solution.py:104
  371.9 7.7 %collective-permute-start.31 = (bf16[800,128]{1,0:T(8,128)(2,1)}, bf16[800,128]{1,0:T(8,128)(2,1)S(1)}, u32[]{:S(2)}, u32[]{:S(2)}) collective-permute-start(bf16[800,128]{1,0:T(8,128)(2,1)} %get-tuple-element.157), channel_id=1, source_target_pairs={{6,0},{7,1},{4,2},{5,3},{2,4},{3,5},{0,6},{1,7},{14,8},{15,9},{12,... | collective-permute-start | bytes 614408 | tf_op jit(solution)/shard_map/ppermute | solution.py:104
  382.2 8.2 %collective-permute-start.32 = (bf16[800,128]{1,0:T(8,128)(2,1)}, bf16[800,128]{1,0:T(8,128)(2,1)S(1)}, u32[]{:S(2)}, u32[]{:S(2)}) collective-permute-start(bf16[800,128]{1,0:T(8,128)(2,1)} %combine.10.refs_0_), channel_id=1, source_target_pairs={{8,0},{9,1},{10,2},{11,3},{12,4},{13,5},{14,6},{15,7},{0,8},{1,9},... | collective-permute-start | bytes 614408 | tf_op jit(solution)/shard_map/ppermute | solution.py:104
  382.3 14.6 %collective-permute-start.33 = (bf16[800,128]{1,0:T(8,128)(2,1)}, bf16[800,128]{1,0:T(8,128)(2,1)}, u32[]{:S(2)}, u32[]{:S(2)}) collective-permute-start(bf16[800,128]{1,0:T(8,128)(2,1)} %combine.10.refs_0_), channel_id=1, source_target_pairs={{16,0},{17,1},{18,2},{19,3},{20,4},{21,5},{22,6},{23,7},{24,8},{25... | collective-permute-start | bytes 614408 | tf_op jit(solution)/shard_map/ppermute | solution.py:104
  382.6 19.9 %collective-permute-start.34 = (bf16[800,128]{1,0:T(8,128)(2,1)}, bf16[800,128]{1,0:T(8,128)(2,1)}, u32[]{:S(2)}, u32[]{:S(2)}) collective-permute-start(bf16[800,128]{1,0:T(8,128)(2,1)} %combine.10.refs_0_), channel_id=1, source_target_pairs={{24,0},{25,1},{26,2},{27,3},{28,4},{29,5},{30,6},{31,7},{16,8},{17... | collective-permute-start | bytes 614408 | tf_op jit(solution)/shard_map/ppermute | solution.py:104
  386.6 33.5 %copy-start.40 = (bf16[512,2048]{1,0:T(8,128)(2,1)S(1)}, bf16[512,2048]{1,0:T(8,128)(2,1)}, u32[]{:S(2)}) copy-start(bf16[512,2048]{1,0:T(8,128)(2,1)} %get-tuple-element.121) | copy-start | bytes 6291460
  389.9 30.2 %copy-start.70 = (f32[1,512]{1,0:T(1,128)S(1)}, f32[1,512]{1,0:T(1,128)}, u32[]{:S(2)}) copy-start(f32[1,512]{1,0:T(1,128)} %get-tuple-element.115) | copy-start | bytes 6148
  389.9 41.4 %collective-permute-start.27 = (bf16[9472,128]{1,0:T(8,128)(2,1)}, bf16[9472,128]{1,0:T(8,128)(2,1)}, u32[]{:S(2)}, u32[]{:S(2)}) collective-permute-start(bf16[9472,128]{1,0:T(8,128)(2,1)} %stack.26.early_own), channel_id=1, source_target_pairs={{1,0},{0,1},{3,2},{2,3},{5,4},{4,5},{7,6},{6,7},{9,8},{8,9},{11,10... | collective-permute-start | bytes 7274504 | tf_op jit(solution)/shard_map/ppermute | solution.py:104
  404.6 7.3 %collective-permute-start.35 = (bf16[800,128]{1,0:T(8,128)(2,1)}, bf16[800,128]{1,0:T(8,128)(2,1)S(1)}, u32[]{:S(2)}, u32[]{:S(2)}) collective-permute-start(bf16[800,128]{1,0:T(8,128)(2,1)} %combine.11.refs_0_), channel_id=1, source_target_pairs={{2,0},{3,1},{0,2},{1,3},{6,4},{7,5},{4,6},{5,7},{10,8},{11,9},{8,1... | collective-permute-start | bytes 614408 | tf_op jit(solution)/shard_map/ppermute | solution.py:104
  405.5 8.2 %collective-permute-start.36 = (bf16[800,128]{1,0:T(8,128)(2,1)}, bf16[800,128]{1,0:T(8,128)(2,1)}, u32[]{:S(2)}, u32[]{:S(2)}) collective-permute-start(bf16[800,128]{1,0:T(8,128)(2,1)} %combine.11.refs_0_), channel_id=1, source_target_pairs={{4,0},{5,1},{6,2},{7,3},{0,4},{1,5},{2,6},{3,7},{12,8},{13,9},{14,... | collective-permute-start | bytes 614408 | tf_op jit(solution)/shard_map/ppermute | solution.py:104
  405.8 10.5 %collective-permute-start.37 = (bf16[800,128]{1,0:T(8,128)(2,1)}, bf16[800,128]{1,0:T(8,128)(2,1)}, u32[]{:S(2)}, u32[]{:S(2)}) collective-permute-start(bf16[800,128]{1,0:T(8,128)(2,1)} %combine.11.refs_0_), channel_id=1, source_target_pairs={{6,0},{7,1},{4,2},{5,3},{2,4},{3,5},{0,6},{1,7},{14,8},{15,9},{12,... | collective-permute-start | bytes 614408 | tf_op jit(solution)/shard_map/ppermute | solution.py:104
  418.5 5.5 %collective-permute-start.38 = (bf16[3200,128]{1,0:T(8,128)(2,1)}, bf16[3200,128]{1,0:T(8,128)(2,1)S(1)}, u32[]{:S(2)}, u32[]{:S(2)}) collective-permute-start(bf16[3200,128]{1,0:T(8,128)(2,1)} %stack.27.late_own.extra_own), channel_id=1, source_target_pairs={{1,0},{0,1},{3,2},{2,3},{5,4},{4,5},{7,6},{6,7},{9,8},{8,9},{11,10... | collective-permute-start | bytes 2457608 | tf_op jit(solution)/shard_map/ppermute | solution.py:104
  418.5 18.0 %collective-permute-start.39 = (bf16[6272,128]{1,0:T(8,128)(2,1)}, bf16[6272,128]{1,0:T(8,128)(2,1)}, u32[]{:S(2)}, u32[]{:S(2)}) collective-permute-start(bf16[6272,128]{1,0:T(8,128)(2,1)} %get-tuple-element.106.refs_0_), channel_id=1, source_target_pairs={{1,0},{0,1},{3,2},{2,3},{5,4},{4,5},{7,6},{6,7},{9,8},{8,9},{11,10... | collective-permute-start | bytes 4816904 | tf_op jit(solution)/shard_map/ppermute | solution.py:104
  419.0 17.5 %collective-permute-start.40 = (bf16[6272,128]{1,0:T(8,128)(2,1)}, bf16[6272,128]{1,0:T(8,128)(2,1)}, u32[]{:S(2)}, u32[]{:S(2)}) collective-permute-start(bf16[6272,128]{1,0:T(8,128)(2,1)} %get-tuple-element.158.refs_1_), channel_id=1, source_target_pairs={{1,0},{0,1},{3,2},{2,3},{5,4},{4,5},{7,6},{6,7},{9,8},{8,9},{11,10... | collective-permute-start | bytes 4816904 | tf_op jit(solution)/shard_map/ppermute | solution.py:104
  419.6 16.9 %collective-permute-start.41 = (bf16[6272,128]{1,0:T(8,128)(2,1)}, bf16[6272,128]{1,0:T(8,128)(2,1)}, u32[]{:S(2)}, u32[]{:S(2)}) collective-permute-start(bf16[6272,128]{1,0:T(8,128)(2,1)} %collective-permute-done.6.refs_4_), channel_id=1, source_target_pairs={{1,0},{0,1},{3,2},{2,3},{5,4},{4,5},{7,6},{6,7},{9,8},{8,9},{11,10... | collective-permute-start | bytes 4816904 | tf_op jit(solution)/shard_map/ppermute | solution.py:104
  423.9 12.6 %collective-permute-start.42 = (bf16[6272,128]{1,0:T(8,128)(2,1)}, bf16[6272,128]{1,0:T(8,128)(2,1)}, u32[]{:S(2)}, u32[]{:S(2)}) collective-permute-start(bf16[6272,128]{1,0:T(8,128)(2,1)} %collective-permute-done.7.refs_5_), channel_id=1, source_target_pairs={{1,0},{0,1},{3,2},{2,3},{5,4},{4,5},{7,6},{6,7},{9,8},{8,9},{11,10... | collective-permute-start | bytes 4816904 | tf_op jit(solution)/shard_map/ppermute | solution.py:104
  (66 other events, 430.9 us)
